TPU v7x, 128 devices: a whole 4x4x4 slice. The times are simulated.
128 devices in a mesh: tile: 16 (over x, z), dp: 8 (over y, core).
Axes of the slice: x: 4, y: 4, z: 4, core: 2. Of those that a mesh axis runs over, the one named last changes fastest.
Arguments:
- features: bfloat16 [1024, 256, 128], P('tile'), may hold values from -6 to 6
- target_field: bfloat16 [1024, 256], P('tile'), may hold values from -3 to 3
- owner_tile: int32 [512, 1], P(('tile', 'dp')), may hold values from 0 to 15; in each aligned block of 4 rows (0 to 3, 4 to 7, ...) at most 2 rows name the same one
- row_offset: int32 [512], P(('tile', 'dp')), may hold values from 0 to 48
- column_start: int32 [512], P(('tile', 'dp')), may hold values from 0 to 240
- noise_level: int32 [512], P(('tile', 'dp')), may hold values from 0 to 31
- icing_count: int32 [512], P(('tile', 'dp')), may hold values from 1 to 4
- noise_draw: float32 [512, 16, 16], P(('tile', 'dp')), may hold values from -6 to 6
- w_a: bfloat16 [1152, 512], replicated, may hold values from -0.1875 to 0.1875
- w_u: float32 [9, 512], replicated, may hold values from -2 to 2
- b_a: float32 [512], replicated, may hold values from -3 to 3
- e_a: float32 [512], replicated, may hold values from -6 to 6
- w_b: bfloat16 [4608, 128], replicated, may hold values from -0.09375 to 0.09375
- b_b: float32 [128], replicated, may hold values from -3 to 3
- w_o: float32 [128], replicated, may hold values from -0.5 to 0.5
Outputs:
- losses: float32 [512], P(('tile', 'dp'))
- upd_a: float32 [512, 1152], P(('tile', 'dp'))
- upd_b: float32 [512, 1152], P(('tile', 'dp'))
Inputs may be any that keep to these rules, and one draw needn't show every extreme that they name: `owner_tile`: among the 4 patches of one device no tile is named more than 2 times, a bound that some block reaches. `row_offset`: a patch's rows lie inside its tile.
All inputs are finite; a program needn't handle non-finite values.
Results may differ from a plain program's by a relative error of at most 0.0027.
Values may be sent and summed in bfloat16 or wider, within the bound.
A program may use at most 128 MiB of HBM per device.

v0:
```python
import math

import jax
import jax.numpy as jnp
from jax import lax
from jax.sharding import PartitionSpec as P

C = 128
HID = 512
P_SIZE = 16
LEVELS = 32


SIGMA_LOW = 0.02
SIGMA_HIGH = 80.0
SIGMA_DATA = 0.5
EPSILON = 1e-06


def silu_prime(values):
    sigmoid_val = jax.nn.sigmoid(values)
    return sigmoid_val * (1.0 + values * (1.0 - sigmoid_val))


def tap_window(padded, shift_row, shift_col, side_len):
    window = padded[:, shift_row : shift_row + side_len, shift_col : shift_col + side_len]
    return window.reshape((-1,) + padded.shape[3:])


def patch_terms(
    patch_feats,
    patch_target,
    noise_draw,
    noise_level,
    icing_count,
    w_a,
    w_u,
    b_a,
    e_a,
    w_b,
    b_b,
    w_o,
):
    npatch = patch_feats.shape[0]
    side_len = patch_feats.shape[1]
    channels = patch_feats.shape[3]
    hidden_width = w_a.shape[1]
    pixels = side_len * side_len
    log_step = (math.log(SIGMA_HIGH) - math.log(SIGMA_LOW)) / (LEVELS - 1)
    sigmas = jnp.exp(math.log(SIGMA_LOW) + noise_level.astype(jnp.float32) * log_step)
    variance = sigmas * sigmas + SIGMA_DATA * SIGMA_DATA
    scale_in = 1.0 / jnp.sqrt(variance)
    scale_skip = SIGMA_DATA * SIGMA_DATA / variance
    scale_out = sigmas * SIGMA_DATA * scale_in
    noise_embed = jnp.log(sigmas) / 4.0
    clean_field = patch_target.astype(jnp.float32)
    noisy_field = clean_field + sigmas[:, None, None] * noise_draw
    aim_value = (
        (clean_field - scale_skip[:, None, None] * noisy_field) / scale_out[:, None, None]
    ).reshape(-1)
    scaled_in = jnp.pad(scale_in[:, None, None] * noisy_field, ((0, 0), (1, 1), (1, 1)))
    feat_pad = jnp.pad(patch_feats, ((0, 0), (1, 1), (1, 1), (0, 0)))
    embed_rows = jnp.repeat(noise_embed, pixels)
    pre_a = b_a[None, :] + embed_rows[:, None] * e_a[None, :]
    for tap_index in range(9):
        shift_row, shift_col = (tap_index // 3, tap_index % 3)
        window = tap_window(feat_pad, shift_row, shift_col, side_len)
        pre_a = pre_a + jnp.dot(
            window,
            w_a[tap_index * channels : (tap_index + 1) * channels],
            preferred_element_type=jnp.float32,
        )
        pre_a = (
            pre_a
            + tap_window(scaled_in, shift_row, shift_col, side_len)[:, None]
            * w_u[tap_index][None, :]
        )
    hidden_act = jax.nn.silu(pre_a).astype(jnp.bfloat16)
    act_pad = jnp.pad(
        hidden_act.reshape(npatch, side_len, side_len, hidden_width),
        ((0, 0), (1, 1), (1, 1), (0, 0)),
    )
    pre_b = jnp.zeros((npatch * pixels, channels), jnp.float32) + b_b[None, :]
    for tap_index in range(9):
        shift_row, shift_col = (tap_index // 3, tap_index % 3)
        window = tap_window(act_pad, shift_row, shift_col, side_len)
        pre_b = pre_b + jnp.dot(
            window,
            w_b[tap_index * hidden_width : (tap_index + 1) * hidden_width],
            preferred_element_type=jnp.float32,
        )
    out_act = jax.nn.silu(pre_b)
    output_map = jnp.dot(out_act, w_o, precision=lax.Precision.HIGHEST)
    residual = output_map - aim_value
    weights = jnp.repeat(icing_count.astype(jnp.float32), pixels)
    losses = jnp.mean((weights * residual * residual).reshape(npatch, pixels), axis=1)
    grad_final = 2.0 * weights * residual / pixels
    grad_pre_b = (grad_final[:, None] * w_o[None, :] * silu_prime(pre_b)).astype(jnp.bfloat16)
    grad_hidden = jnp.zeros((npatch, side_len + 2, side_len + 2, hidden_width), jnp.float32)
    parts_b = []
    for tap_index in range(9):
        shift_row, shift_col = (tap_index // 3, tap_index % 3)
        window = tap_window(act_pad, shift_row, shift_col, side_len)
        parts_b.append(
            lax.dot_general(
                window, grad_pre_b, (((0,), (0,)), ((), ())), preferred_element_type=jnp.float32
            )
        )
        back_term = lax.dot_general(
            grad_pre_b,
            w_b[tap_index * hidden_width : (tap_index + 1) * hidden_width],
            (((1,), (1,)), ((), ())),
            preferred_element_type=jnp.float32,
        )
        grad_hidden = grad_hidden.at[
            :, shift_row : shift_row + side_len, shift_col : shift_col + side_len
        ].add(back_term.reshape(npatch, side_len, side_len, hidden_width))
    grad_pre_a = (grad_hidden[:, 1:-1, 1:-1].reshape(-1, hidden_width) * silu_prime(pre_a)).astype(
        jnp.bfloat16
    )
    parts_a = []
    for tap_index in range(9):
        shift_row, shift_col = (tap_index // 3, tap_index % 3)
        window = tap_window(feat_pad, shift_row, shift_col, side_len)
        parts_a.append(
            lax.dot_general(
                grad_pre_a, window, (((0,), (0,)), ((), ())), preferred_element_type=jnp.float32
            )
        )
    return (losses, jnp.concatenate(parts_a, axis=1), jnp.concatenate(parts_b, axis=1))


def local(
    features,
    target_field,
    owner_tile,
    row_offset,
    column_start,
    noise_level,
    icing_count,
    noise_draw,
    w_a,
    w_u,
    b_a,
    e_a,
    w_b,
    b_b,
    w_o,
):
    tile_count = lax.axis_size("tile")
    npatch = owner_tile.shape[0]
    slot_cap = max(2, 2 * npatch // tile_count)
    slot_total = tile_count * slot_cap
    owner_index = owner_tile[:, 0]
    position = jnp.arange(npatch, dtype=jnp.int32)
    same_owner = (owner_index[None, :] == owner_index[:, None]) & (
        position[None, :] < position[:, None]
    )
    slot_rank = jnp.sum(same_owner.astype(jnp.int32), axis=1)
    slot_key = owner_index * slot_cap + slot_rank
    selector = (slot_key[None, :] == jnp.arange(slot_total, dtype=jnp.int32)[:, None]).astype(
        jnp.int32
    )

    def extract(source_row, source_col):
        anchor = jnp.zeros((), jnp.int32)
        feat_block = lax.dynamic_slice(
            features, (source_row, source_col, anchor), (P_SIZE, P_SIZE, C)
        )
        target_block = lax.dynamic_slice(target_field, (source_row, source_col), (P_SIZE, P_SIZE))
        return (feat_block, target_block)

    wanted = jnp.stack([row_offset, column_start], axis=1)
    request_table = jnp.sum(selector[:, :, None] * wanted[None, :, :], axis=1).reshape(
        tile_count, slot_cap, 2
    )
    request = lax.all_to_all(request_table, "tile", split_axis=0, concat_axis=0, tiled=True)
    slot_width = request.shape[1]
    flat_table = request.reshape(-1, 2)
    blocks, fields = jax.vmap(extract)(flat_table[:, 0], flat_table[:, 1])
    blocks = blocks.reshape(tile_count, slot_width, P_SIZE, P_SIZE, C)
    fields = fields.reshape(tile_count, slot_width, P_SIZE, P_SIZE)
    fetched = lax.all_to_all(blocks, "tile", split_axis=0, concat_axis=0, tiled=True)
    fetched_target = lax.all_to_all(fields, "tile", split_axis=0, concat_axis=0, tiled=True)
    patch_feats = fetched.reshape(slot_total, P_SIZE, P_SIZE, C)[slot_key]
    patch_target = fetched_target.reshape(slot_total, P_SIZE, P_SIZE)[slot_key]
    losses, grad_a, grad_b = patch_terms(
        patch_feats,
        patch_target,
        noise_draw,
        noise_level,
        icing_count,
        w_a,
        w_u,
        b_a,
        e_a,
        w_b,
        b_b,
        w_o,
    )
    combined = jnp.concatenate([grad_a, grad_b], axis=1)
    owned_rows = lax.psum_scatter(combined, ("tile", "dp"), scatter_dimension=0, tiled=True)
    tap_width = 9 * C
    shard_a = owned_rows[:, :tap_width]
    shard_b = owned_rows[:, tap_width:]
    squares = lax.psum((jnp.sum(shard_a * shard_a), jnp.sum(shard_b * shard_b)), ("tile", "dp"))
    count_all = HID * tap_width
    upd_a = shard_a / jnp.sqrt(squares[0] / count_all + EPSILON)
    upd_b = shard_b / jnp.sqrt(squares[1] / count_all + EPSILON)
    return (losses, upd_a, upd_b)


def solution(mesh):
    return jax.shard_map(
        local,
        mesh=mesh,
        in_specs=(
            P("tile", None, None),
            P("tile", None),
            P(("tile", "dp"), None),
            P(("tile", "dp")),
            P(("tile", "dp")),
            P(("tile", "dp")),
            P(("tile", "dp")),
            P(("tile", "dp"), None, None),
            P(),
            P(),
            P(),
            P(),
            P(),
            P(),
            P(),
        ),
        out_specs=(P(("tile", "dp")), P(("tile", "dp"), None), P(("tile", "dp"), None)),
        check_vma=False,
    )
```

profile of v0, /device:TPU:1, one launch (start us, length us, event | category | flops | bytes accessed | tf_op | source)
XLA Modules:
  0.0 624.0 jit_solution(16252502467898229803)
XLA Ops:
  10.3 8.4 %all-to-all-start = ((s32[16,2,2]{1,2,0:T(2,128)}), s32[16,2,2]{1,2,0:T(2,128)S(1)}, u32[]{:S(2)}, u32[]{:S(2)}) async-start(s32[16,2,2]{1,2,0:T(2,128)} %copy.29), calls=%async_computation | async-start | bytes 32768 | tf_op jit(solution)/shard_map/all_to_all | solution.py:177
  19.4 5.8 all-to-all-done
  25.3 83.1 %while.12 = (s32[]{:T(128)}, bf16[64,256]{1,0:T(8,128)(2,1)}, s32[32,2]{0,1:T(2,128)S(1)}, bf16[32,16,16]{2,1,0:T(8,128)(2,1)S(1)}, s32[]{:T(128)}) while((s32[]{:T(128)}, bf16[64,256]{1,0:T(8,128)(2,1)}, s32[32,2]{0,1:T(2,128)S(1)}, bf16[32,16,16]{2,1,0:T(8,128)(2,1)S(1)}, s32[]{:T(128)}) %tuple.117), condition=%wide.while_cond.10, body=%wide.while_body.10.sunk | while | flops 2 | bytes 4717 | solution.py:170
  109.2 3.5 all-to-all-start.2
  112.7 107.3 %while.11 = (s32[]{:T(128)}, bf16[64,256,128]{2,1,0:T(8,128)(2,1)}, s32[32,3]{0,1:T(4,128)S(1)}, bf16[32,16,16,128]{3,2,1,0:T(8,128)(2,1)}, s32[]{:T(128)}) while((s32[]{:T(128)}, bf16[64,256,128]{2,1,0:T(8,128)(2,1)}, s32[32,3]{0,1:T(4,128)S(1)}, bf16[32,16,16,128]{3,2,1,0:T(8,128)(2,1)}, s32[]{:T(128)}) %tuple.120), condition=%wide.while_cond.9, body=%wide.while_body.9.sunk | while | flops 2 | bytes 132713 | solution.py:167
  113.3 2.8 bitcast_dynamic-update-slice_fusion.4
  120.0 2.8 bitcast_dynamic-update-slice_fusion.4
  123.3 2.8 bitcast_dynamic-update-slice_fusion.4
  126.7 2.8 bitcast_dynamic-update-slice_fusion.4
  130.1 2.8 bitcast_dynamic-update-slice_fusion.4
  133.4 2.8 bitcast_dynamic-update-slice_fusion.4
  136.8 2.8 bitcast_dynamic-update-slice_fusion.4
  140.1 2.8 bitcast_dynamic-update-slice_fusion.4
  143.5 2.8 bitcast_dynamic-update-slice_fusion.4
  146.8 2.8 bitcast_dynamic-update-slice_fusion.4
  150.2 2.8 bitcast_dynamic-update-slice_fusion.4
  153.5 2.8 bitcast_dynamic-update-slice_fusion.4
  156.9 2.8 bitcast_dynamic-update-slice_fusion.4
  160.2 2.8 bitcast_dynamic-update-slice_fusion.4
  163.6 2.8 bitcast_dynamic-update-slice_fusion.4
  166.9 2.8 bitcast_dynamic-update-slice_fusion.4
  170.3 2.8 bitcast_dynamic-update-slice_fusion.4
  173.6 2.8 bitcast_dynamic-update-slice_fusion.4
  180.3 2.8 bitcast_dynamic-update-slice_fusion.4
  187.0 2.8 bitcast_dynamic-update-slice_fusion.4
  190.4 2.8 bitcast_dynamic-update-slice_fusion.4
  193.7 2.8 bitcast_dynamic-update-slice_fusion.4
  200.5 2.8 bitcast_dynamic-update-slice_fusion.4
  203.8 2.8 bitcast_dynamic-update-slice_fusion.4
  207.2 2.8 bitcast_dynamic-update-slice_fusion.4
  210.5 2.8 bitcast_dynamic-update-slice_fusion.4
  213.9 2.8 bitcast_dynamic-update-slice_fusion.4
  217.2 2.8 bitcast_dynamic-update-slice_fusion.4
  220.0 6.7 %all-to-all-start.1 = ((bf16[16,2,16,16,128]{4,3,2,1,0:T(8,128)(2,1)}), bf16[16,2,16,16,128]{4,3,2,1,0:T(8,128)(2,1)S(1)}, u32[]{:S(2)}, u32[]{:S(2)}) async-start(bf16[16,2,16,16,128]{4,3,2,1,0:T(8,128)(2,1)} %bitcast.201), calls=%async_computation.1 | async-start | bytes 4194304 | tf_op jit(solution)/shard_map/all_to_all | solution.py:183
  238.7 13.3 %all-to-all-done.1 = bf16[16,2,16,16,128]{4,3,2,1,0:T(8,128)(2,1)S(1)} async-done(((bf16[16,2,16,16,128]{4,3,2,1,0:T(8,128)(2,1)}), bf16[16,2,16,16,128]{4,3,2,1,0:T(8,128)(2,1)S(1)}, u32[]{:S(2)}, u32[]{:S(2)}) %all-to-all-start.1) | async-done | bytes 2097184 | tf_op jit(solution)/shard_map/all_to_all | solution.py:183
  256.9 4.6 multiply_convert_fusion
  283.0 3.1 dynamic-slice_add_fusion
  286.1 10.5 %scatter-add.31 = f32[4,18,18,512]{3,2,1,0:T(8,128)S(1)} dynamic-update-slice(f32[4,18,18,512]{3,2,1,0:T(8,128)S(1)} %scatter-add.30, f32[4,16,16,512]{3,2,1,0:T(8,128)} %dynamic-slice_add_fusion, s32[]{:T(128)} %constant.298.clone.1, s32[]{:T(128)} %bitcast.39, s32[]{:T(128)} %bitcast.40, s32[]{:T(128)} %constant.298.clone.1) | dynamic-update-slice | bytes 4194308 | tf_op jit(solution)/shard_map/scatter-add | solution.py:117
  296.6 5.6 add_select_fusion
  302.2 10.7 %scatter-add.34 = f32[4,18,18,512]{3,2,1,0:T(8,128)S(1)} dynamic-update-slice(f32[4,18,18,512]{3,2,1,0:T(8,128)S(1)} %scatter-add.31, f32[4,16,16,512]{3,2,1,0:T(8,128)} %add_select_fusion, s32[]{:T(128)} %constant.298.clone.1, s32[]{:T(128)} %bitcast.42, s32[]{:T(128)} %bitcast.43, s32[]{:T(128)} %constant.298.clone.1) | dynamic-update-slice | bytes 4194308 | tf_op jit(solution)/shard_map/scatter-add | solution.py:117
  317.3 9.2 %scatter-add.36 = f32[4,18,18,512]{3,2,1,0:T(8,128)S(1)} dynamic-update-slice(f32[4,18,18,512]{3,2,1,0:T(8,128)S(1)} %fusion.1, f32[4,16,16,512]{3,2,1,0:T(8,128)} %slice_add_fusion.4, s32[]{:T(128)} %constant.298.clone.1, s32[]{:T(128)} %constant.311.clone.1, s32[]{:T(128)} %constant.311.clone.1, s32[]{:T(128)} %constant.298.clone.1) | dynamic-update-slice | bytes 4194308 | tf_op jit(solution)/shard_map/scatter-add | solution.py:117
  326.6 3.7 slice_add_fusion.3
  330.3 9.2 %scatter-add.39 = f32[4,18,18,512]{3,2,1,0:T(8,128)S(1)} dynamic-update-slice(f32[4,18,18,512]{3,2,1,0:T(8,128)S(1)} %scatter-add.36, f32[4,16,16,512]{3,2,1,0:T(8,128)} %slice_add_fusion.3, s32[]{:T(128)} %constant.298.clone.1, s32[]{:T(128)} %constant.311.clone.1, s32[]{:T(128)} %constant.297.clone.1, s32[]{:T(128)} %constant.298.clone.1) | dynamic-update-slice | bytes 4194308 | tf_op jit(solution)/shard_map/scatter-add | solution.py:117
  343.8 9.2 %scatter-add.41 = f32[4,18,18,512]{3,2,1,0:T(8,128)S(1)} dynamic-update-slice(f32[4,18,18,512]{3,2,1,0:T(8,128)S(1)} %fusion, f32[4,16,16,512]{3,2,1,0:T(8,128)} %slice_add_fusion.1, s32[]{:T(128)} %constant.298.clone.1, s32[]{:T(128)} %constant.297.clone.1, s32[]{:T(128)} %constant.311.clone.1, s32[]{:T(128)} %constant.298.clone.1) | dynamic-update-slice | bytes 4194308 | tf_op jit(solution)/shard_map/scatter-add | solution.py:117
  353.0 3.6 slice_add_fusion
  356.6 9.2 %scatter-add.44 = f32[4,18,18,512]{3,2,1,0:T(8,128)S(1)} dynamic-update-slice(f32[4,18,18,512]{3,2,1,0:T(8,128)S(1)} %scatter-add.41, f32[4,16,16,512]{3,2,1,0:T(8,128)} %slice_add_fusion, s32[]{:T(128)} %constant.298.clone.1, s32[]{:T(128)} %constant.297.clone.1, s32[]{:T(128)} %constant.297.clone.1, s32[]{:T(128)} %constant.298.clone.1) | dynamic-update-slice | bytes 4194308 | tf_op jit(solution)/shard_map/scatter-add | solution.py:117
  388.2 158.0 %all-reduce.8.cloned.1.call-done = f32[512,2304]{0,1:T(8,128)} async-done(((f32[512,2304]{0,1:T(8,128)}), f32[512,2304]{0,1:T(8,128)}) %all-reduce.8.cloned.1.call-update) | async-done | bytes 4718608
  548.4 64.1 %all-reduce.5 = (f32[]{:T(128)}, f32[]{:T(128)}) all-reduce(f32[]{:T(128)} %get-tuple-element.140, f32[]{:T(128)} %get-tuple-element.139), channel_id=1, replica_groups=mesh['tile'=16,'dp'=8] {'tile','dp'}, use_global_device_ids=true, to_apply=%region_6.7 | all-reduce | flops 2 | bytes 16 | tf_op jit(solution)/shard_map/psum | solution.py:206
  (416 shorter events, 191.7 us)
Async XLA Ops:
  10.3 14.9 %all-to-all-start = ((s32[16,2,2]{1,2,0:T(2,128)}), s32[16,2,2]{1,2,0:T(2,128)S(1)}, u32[]{:S(2)}, u32[]{:S(2)}) async-start(s32[16,2,2]{1,2,0:T(2,128)} %copy.29), calls=%async_computation | async-start | bytes 32768 | tf_op jit(solution)/shard_map/all_to_all | solution.py:177
  109.2 110.8 %all-to-all-start.2 = ((bf16[16,2,256]{2,1,0:T(2,128)(2,1)}), bf16[16,2,256]{2,1,0:T(2,128)(2,1)S(1)}, u32[]{:S(2)}, u32[]{:S(2)}) async-start(bf16[16,2,256]{2,1,0:T(2,128)(2,1)} %reshape.648), calls=%async_computation.2 | async-start | bytes 32768 | tf_op jit(solution)/shard_map/all_to_all | solution.py:184
  220.0 7.5 %copy-start.68 = (s32[4]{0:T(128)S(1)}, s32[4]{0:T(128)}, u32[]{:S(2)}) copy-start(s32[4]{0:T(128)} %param.39) | copy-start | bytes 52
  220.0 7.6 %copy-start.69 = (s32[4,1]{0,1:T(1,128)S(1)}, s32[4,1]{0,1:T(1,128)}, u32[]{:S(2)}) copy-start(s32[4,1]{0,1:T(1,128)} %param.35) | copy-start | bytes 52
  220.0 8.9 %copy-start.64 = (s32[4]{0:T(128)S(1)}, s32[4]{0:T(128)}, u32[]{:S(2)}) copy-start(s32[4]{0:T(128)} %constant.309.clone.1) | copy-start | bytes 52
  220.0 9.6 %copy-start.44 = (f32[9,512]{1,0:T(8,128)S(1)}, f32[9,512]{1,0:T(8,128)}, u32[]{:S(2)}) copy-start(f32[9,512]{1,0:T(8,128)} %param.42) | copy-start | bytes 55300
  220.0 10.9 %copy-start.43 = (f32[4,16,16]{2,1,0:T(8,128)S(1)}, f32[4,16,16]{2,1,0:T(8,128)}, u32[]{:S(2)}) copy-start(f32[4,16,16]{2,1,0:T(8,128)} %param.40) | copy-start | bytes 12292
  220.0 32.0 %all-to-all-start.1 = ((bf16[16,2,16,16,128]{4,3,2,1,0:T(8,128)(2,1)}), bf16[16,2,16,16,128]{4,3,2,1,0:T(8,128)(2,1)S(1)}, u32[]{:S(2)}, u32[]{:S(2)}) async-start(bf16[16,2,16,16,128]{4,3,2,1,0:T(8,128)(2,1)} %bitcast.201), calls=%async_computation.1 | async-start | bytes 4194304 | tf_op jit(solution)/shard_map/all_to_all | solution.py:183
  226.8 26.3 %copy-start.42 = (bf16[1152,512]{1,0:T(8,128)(2,1)S(1)}, bf16[1152,512]{1,0:T(8,128)(2,1)}, u32[]{:S(2)}) copy-start(bf16[1152,512]{1,0:T(8,128)(2,1)} %param.41) | copy-start | bytes 3538948
  226.8 319.4 %all-reduce.8.cloned.1.call-start = ((), (), s32[]{:S(2)}) async-start(), calls=%async_computation.3 | async-start | bytes 9437184
  252.6 3.6 copy-start.23
  253.0 1.8 copy-start.37
  253.0 2.2 copy-start.25
  253.0 2.6 copy-start.27
  253.1 3.6 copy-start.40
  261.5 4.6 copy-start.4
  261.5 2.8 copy-start.22
  261.5 2.8 copy-start.63
  264.2 1.4 copy-start.2
  264.2 2.3 copy-start.12
  264.2 2.7 copy-start.14
  264.3 2.7 copy-start.16
  264.3 2.7 copy-start.18
  264.3 2.7 copy-start.10
  264.3 3.2 copy-start.8
  264.3 3.6 copy-start.6
  269.3 11.6 %copy-start = (bf16[1024,128]{1,0:T(8,128)(2,1)}, bf16[1024,128]{1,0:T(8,128)(2,1)S(1)}, u32[]{:S(2)}) copy-start(bf16[1024,128]{1,0:T(8,128)(2,1)S(1)} %multiply_convert_fusion.1) | copy-start | bytes 786436
  312.9 2.3 copy-start.21
  339.5 2.3 copy-start.20
  365.8 1.6 copy-start.39
  367.4 2.0 copy-start.36
  368.4 2.1 copy-start.34
  368.4 3.2 copy-start.32
  369.4 3.2 copy-start.24
  370.5 3.2 copy-start.30
  371.6 3.2 copy-start.28
  372.6 3.2 copy-start.26
  373.7 3.2 copy-start.41
  374.8 3.2 copy-start.1
  374.8 3.2 copy-start.3
  375.8 3.2 copy-start.19
  376.9 3.2 copy-start.17
  377.9 3.2 copy-start.15
  379.0 3.2 copy-start.5
  380.1 3.2 copy-start.13
  381.1 3.2 copy-start.11
  382.2 3.2 copy-start.9
  383.2 3.2 copy-start.7
  (26 other events, 27.3 us)
Sparse Core Ops, SparseCore 0:
  387.6 158.4 all-reduce.7
where the time goes:
time: 629 us; the launch traced here: 624 us
  local copies, waits for them, and re-layouts  269 us (43%)
  waiting for transfers between devices  177 us (28%)
  blocking collectives  64.1 us (10%)
  matrix products  44.8 us (7%)
  other arithmetic  34.1 us (5%)
  starting transfers between devices  18.7 us (3%)
  between operations  16.5 us (3%)
    gather x192, local copies, waits for them, and re-layouts  190 us
    unnamed x2, waiting for transfers between devices  158 us
    psum x1, blocking collectives, local(): lax.psum((jnp.sum(shard_a * shard_a), jnp.sum(shard_b * shard_b)), ('tile...  64.1 us
    scatter-add x7, local copies, waits for them, and re-layouts, patch_terms(): grad_hidden = grad_hidden.at[:, shift_row:shift_row + side_len, shift_col...  58.4 us
    add x5, other arithmetic, patch_terms(): grad_hidden = grad_hidden.at[:, shift_row:shift_row + side_len, shift_col...  14.5 us
    dot_general x9, matrix products, patch_terms(): lax.dot_general(grad_pre_b, w_b[tap_index * hidden_width:(tap_index + 1)...  13.3 us
    all_to_all x1, waiting for transfers between devices, local(): lax.all_to_all(blocks, 'tile', split_axis=0, concat_axis=0, tiled=True)  13.3 us
  transfers between devices with their start and end apart: 4, of which 3 were waited for; matrix products, arithmetic and copies ran while one was open for 19% of the time, Pallas kernels for 0%

commit v1 on v0

v1 whole, which is shorter than its diff:
```python
import functools
import math

import jax
import jax.numpy as jnp
from jax import lax
from jax.experimental import pallas as pl
from jax.experimental.pallas import tpu as pltpu
from jax.sharding import PartitionSpec as P

C = 128
HID = 512
SIDE = 16
LEVELS = 32
NP = 4
CELLS = SIDE * SIDE
TAPS = 9
WIDE = TAPS * C
SIGMA_LOW = 0.02
SIGMA_HIGH = 80.0
SIGMA_DATA = 0.5
EPSILON = 1e-06
LOG_LOW = math.log(SIGMA_LOW)
LOG_STEP = (math.log(SIGMA_HIGH) - math.log(SIGMA_LOW)) / (LEVELS - 1)

MESH = pl.DeviceIdType.MESH
F32 = jnp.float32
BF16 = jnp.bfloat16
N_TILE = 16
N_DP = 8
AX = 4
PART = WIDE // 3


def iota(shape, dim):
    return lax.broadcasted_iota(jnp.int32, shape, dim)


def remote(src, dst, send_sem, recv_sem, tile, dp):
    return pltpu.make_async_remote_copy(
        src_ref=src,
        dst_ref=dst,
        send_sem=send_sem,
        recv_sem=recv_sem,
        device_id=(tile, dp),
        device_id_type=MESH,
    )


def column_shifts(block):
    col = iota(block.shape, 1)
    before = jnp.where(col == 0, 0.0, pltpu.roll(block, 1, axis=1))
    after = jnp.where(col == SIDE - 1, 0.0, pltpu.roll(block, SIDE - 1, axis=1))
    return before, block, after


def store_rows(dst, p, lane, rows, delta):
    lanes = slice(lane, lane + C)
    base = p * SIDE
    zero = jnp.zeros((1, SIDE, C), BF16)
    if delta == 0:
        dst[base : base + SIDE, :, lanes] = rows
    elif delta < 0:
        dst[base : base + 1, :, lanes] = zero
        dst[base + 1 : base + SIDE, :, lanes] = rows[: SIDE - 1]
    else:
        dst[base : base + SIDE - 1, :, lanes] = rows[1:]
        dst[base + SIDE - 1 : base + SIDE, :, lanes] = zero


def kernel(
    feat_hbm,
    tgt_ref,
    owner_ref,
    row_ref,
    col_ref,
    level_ref,
    count_ref,
    noise_ref,
    wa_hbm,
    wu_ref,
    ba_ref,
    ea_ref,
    wb_hbm,
    bb_ref,
    wo_ref,
    losses_ref,
    upda_ref,
    updb_ref,
    feat_v,
    feat_f,
    tgt_v,
    req_send,
    req_recv,
    req_smem,
    slots,
    landed,
    blk,
    noise_v,
    wfull,
    wext,
    w2,
    xcol,
    gcol,
    act,
    slope,
    gpa,
    mine,
    theirs,
    sib_recv,
    s1_send,
    s1_recv,
    s2_send,
    s2_recv,
    s3_send,
    s3_recv,
    fin_send,
    fin_recv,
    nrm_send,
    nrm_recv,
    nrm2_send,
    nrm2_recv,
    local_sem,
    req_ssem,
    req_rsem,
    slot_ssem,
    slot_rsem,
    sib_sem,
    s1_ssem,
    s1_rsem,
    s2_ssem,
    s2_rsem,
    s3_ssem,
    s3_rsem,
    fin_sem,
    n1_ssem,
    n1_rsem,
    n2_ssem,
    n2_rsem,
):
    me_t = lax.axis_index("tile")
    me_d = lax.axis_index("dp")
    x, z = me_t // AX, me_t % AX
    y, core = me_d // 2, me_d % 2

    def tile_peer(o):
        return ((x + o // AX) % AX) * AX + (z + o % AX) % AX

    def dp_peer(o):
        return (me_d + o) % N_DP

    barrier = pltpu.get_barrier_semaphore()

    @pl.loop(1, N_TILE)
    def _(o):
        pl.semaphore_signal(barrier, inc=1, device_id=(tile_peer(o), me_d), device_id_type=MESH)

    @pl.loop(1, N_DP)
    def _(o):
        pl.semaphore_signal(barrier, inc=1, device_id=(me_t, dp_peer(o)), device_id_type=MESH)

    feat_copy = pltpu.make_async_copy(feat_hbm, feat_v, local_sem.at[0])
    feat_copy.start()
    wa_copy = pltpu.make_async_copy(wa_hbm, wfull.at[pl.ds(0, WIDE)], local_sem.at[1])
    wa_copy.start()
    wb_copies = [
        pltpu.make_async_copy(
            wb_hbm.at[pl.ds(t * HID, HID)], w2.at[:, pl.ds(t * C, C)], local_sem.at[2 + t]
        )
        for t in range(TAPS)
    ]
    for copy in wb_copies:
        copy.start()

    lane = iota((1, C), 1)
    line = jnp.zeros((1, C), jnp.int32)
    for k in range(NP):
        line = jnp.where(lane == 4 * k, owner_ref[k, 0], line)
        line = jnp.where(lane == 4 * k + 1, row_ref[k], line)
        line = jnp.where(lane == 4 * k + 2, col_ref[k], line)
    req_send[...] = line
    req_recv[me_t] = line
    tgt_v[0] = tgt_ref[:, :C].astype(F32)
    tgt_v[1] = tgt_ref[:, C:].astype(F32)
    pl.semaphore_wait(barrier, N_TILE - 1 + N_DP - 1)

    def req_copy(o):
        return remote(
            req_send, req_recv.at[me_t], req_ssem.at[o], req_rsem.at[o], tile_peer(o), me_d
        )

    @pl.loop(1, N_TILE)
    def _(o):
        req_copy(o).start()

    feat_copy.wait()

    @pl.loop(0, 64)
    def _(i):
        feat_f[i] = feat_v[i].astype(F32)

    @pl.loop(1, N_TILE)
    def _(o):
        req_copy(o).wait()

    to_smem = pltpu.make_async_copy(req_recv, req_smem, local_sem.at[2 + TAPS])
    to_smem.start()
    to_smem.wait()

    def cut(row, col):
        block = feat_f[pl.ds(row, SIDE), pl.ds(col, SIDE), :]
        rows = jnp.concatenate([tgt_v[i, pl.ds(row, SIDE), :] for i in range(2)], axis=1)
        shift = jnp.full(rows.shape, col, jnp.int32)
        for bit in (1, 2, 4, 8, 16, 32, 64, 128):
            rows = jnp.where((shift & bit) != 0, pltpu.roll(rows, 256 - bit, axis=1), rows)
        return block.astype(BF16), rows[:, :C].astype(BF16)

    def fill(dst, j):
        rank = jnp.int32(0)
        rows = [jnp.int32(0), jnp.int32(0)]
        cols = [jnp.int32(0), jnp.int32(0)]
        for k in range(NP):
            hit = req_smem[j, 0, 4 * k] == me_t
            for q in range(2):
                take = hit & (rank == q)
                rows[q] = jnp.where(take, req_smem[j, 0, 4 * k + 1], rows[q])
                cols[q] = jnp.where(take, req_smem[j, 0, 4 * k + 2], cols[q])
            rank = rank + hit.astype(jnp.int32)
        for q in range(2):
            block, field = cut(rows[q], cols[q])
            dst[q, :SIDE] = block
            dst[q, SIDE] = field

    def slot_copy(o):
        return remote(
            slots.at[o], landed.at[me_t], slot_ssem.at[o], slot_rsem.at[o], tile_peer(o), me_d
        )

    @pl.loop(1, N_TILE)
    def _(i):
        o = (i * 5) % N_TILE
        fill(slots.at[o], tile_peer(o))
        slot_copy(o).start()

    fill(landed.at[me_t], me_t)

    wa_copy.wait()
    for copy in wb_copies:
        copy.wait()
    wu = wu_ref[...]
    wu_hi = wu.astype(BF16).astype(F32)
    ba = ba_ref[...].reshape(1, HID)
    ba_hi = ba.astype(BF16).astype(F32)
    ea = ea_ref[...].reshape(1, HID)
    ea_hi = ea.astype(BF16).astype(F32)
    wext[...] = jnp.zeros_like(wext)
    wext[0:9] = wu_hi
    wext[9:18] = wu - wu_hi
    wext[18:27] = wu_hi
    wext[27:28] = ba_hi
    wext[28:29] = ba - ba_hi
    wext[29:30] = ea_hi
    wext[30:31] = ea - ea_hi
    wext[31:32] = ea_hi
    wfull[WIDE:, :] = wext[...].astype(BF16)
    noise_v[...] = jnp.zeros_like(noise_v)
    noise_v[:, :, 0:SIDE] = noise_ref[...]

    @pl.loop(1, N_TILE)
    def _(o):
        slot_copy(o).wait()

    owners = [owner_ref[k, 0] for k in range(NP)]
    for k in range(NP):
        rank = jnp.int32(0)
        for before in range(k):
            rank = rank + (owners[before] == owners[k]).astype(jnp.int32)
        blk[k] = landed[owners[k], jnp.minimum(rank, 1)]

    wo = wo_ref[...].reshape(1, 1, C)
    bb = bb_ref[...].reshape(1, 1, C)
    shape3 = (SIDE, SIDE, C)
    col3, lane3 = iota(shape3, 1), iota(shape3, 2)
    lane2 = iota((SIDE, C), 1)
    for p in range(NP):
        block = blk[p, :SIDE].astype(F32)
        for s, moved in enumerate(column_shifts(block)):
            rows = moved.astype(BF16)
            for r in range(3):
                store_rows(xcol, p, (3 * r + s) * C, rows, r - 1)

        level = jnp.full((SIDE, C), level_ref[p], jnp.int32).astype(F32)
        sigma = jnp.exp(LOG_LOW + level * LOG_STEP)
        variance = sigma * sigma + SIGMA_DATA * SIGMA_DATA
        scale_in = 1.0 / jnp.sqrt(variance)
        scale_skip = SIGMA_DATA * SIGMA_DATA / variance
        scale_out = sigma * SIGMA_DATA * scale_in
        embed = jnp.log(sigma) / 4.0
        clean = jnp.where(lane2 < SIDE, blk[p, SIDE].astype(F32), 0.0)
        noisy = clean + sigma * noise_v[p]
        aim = (clean - scale_skip * noisy) / scale_out
        scaled = pltpu.roll(scale_in * noisy, 1, axis=1)
        wide = jnp.broadcast_to(scaled[:, None, :], shape3)
        for bit in (1, 2, 4, 8):
            wide = jnp.where((col3 & bit) != 0, pltpu.roll(wide, C - bit, axis=2), wide)
        wide = jnp.where(lane3 < 3, wide, 0.0)
        none = jnp.zeros((1, SIDE, C), F32)
        taps = (
            jnp.concatenate([none, wide[: SIDE - 1]], axis=0)
            + pltpu.roll(wide, 3, axis=2)
            + pltpu.roll(jnp.concatenate([wide[1:], none], axis=0), 6, axis=2)
        )
        taps_hi = taps.astype(BF16).astype(F32)
        emb = embed[0:1, :][None]
        emb_hi = emb.astype(BF16).astype(F32)
        extra = taps_hi + pltpu.roll(taps_hi, 9, axis=2) + pltpu.roll(taps - taps_hi, 18, axis=2)
        extra = jnp.where((lane3 == 27) | (lane3 == 28), 1.0, extra)
        extra = jnp.where((lane3 == 29) | (lane3 == 30), emb_hi, extra)
        extra = jnp.where(lane3 == 31, emb - emb_hi, extra)
        xcol[p * SIDE : (p + 1) * SIDE, :, WIDE:] = extra.astype(BF16)

        cells = slice(p * CELLS, (p + 1) * CELLS)
        window = xcol[p * SIDE : (p + 1) * SIDE].reshape(CELLS, WIDE + C)
        pre_a = jnp.dot(window, wfull[...], preferred_element_type=F32)
        gate = jax.nn.sigmoid(pre_a)
        slope[cells] = gate * (1.0 + pre_a * (1.0 - gate))
        hidden = (pre_a * gate).astype(BF16)
        act[cells] = hidden

        spread = jnp.dot(hidden, w2[...], preferred_element_type=F32).reshape(SIDE, SIDE, WIDE)

        def tap_rows(s):
            up = spread[:, :, s * C : (s + 1) * C]
            mid = spread[:, :, (3 + s) * C : (4 + s) * C]
            down = spread[:, :, (6 + s) * C : (7 + s) * C]
            return (
                mid
                + jnp.concatenate([none, up[: SIDE - 1]], axis=0)
                + jnp.concatenate([down[1:], none], axis=0)
            )

        left = jnp.where(col3 == 0, 0.0, pltpu.roll(tap_rows(0), 1, axis=1))
        right = jnp.where(col3 == SIDE - 1, 0.0, pltpu.roll(tap_rows(2), SIDE - 1, axis=1))
        pre_b = bb + tap_rows(1) + left + right
        gate_b = jax.nn.sigmoid(pre_b)
        aim3 = jnp.where(col3 == lane3, jnp.broadcast_to(aim[:, None, :], shape3), 0.0)
        residual = jnp.sum(pre_b * gate_b * wo - aim3, axis=2, keepdims=True)
        weight = count_ref[p].astype(F32)
        losses_ref[p] = jnp.sum(residual * residual) * weight / CELLS
        grad_final = (2.0 * weight / CELLS) * residual
        grad_b = grad_final * wo * (gate_b * (1.0 + pre_b * (1.0 - gate_b)))
        grad_b = grad_b.astype(BF16).astype(F32)
        for s, moved in enumerate(column_shifts(grad_b)):
            rows = moved.astype(BF16)
            for r in range(3):
                store_rows(gcol, p, (3 * (2 - r) + (2 - s)) * C, rows, r - 1)

        back = lax.dot_general(
            gcol[p * SIDE : (p + 1) * SIDE].reshape(CELLS, WIDE),
            w2[...],
            (((1,), (1,)), ((), ())),
            preferred_element_type=F32,
        )
        gpa[cells] = (back * slope[cells]).astype(BF16)

    over_cells = (((0,), (0,)), ((), ()))
    for part in range(3):
        lanes = slice(part * PART, (part + 1) * PART)
        grad_a = lax.dot_general(
            gpa[...],
            xcol[:, :, lanes].reshape(NP * CELLS, PART),
            over_cells,
            preferred_element_type=F32,
        )
        grad_b = lax.dot_general(
            act[...],
            gcol[:, :, lanes].reshape(NP * CELLS, PART),
            over_cells,
            preferred_element_type=F32,
        )
        first = core == 0
        mine[:, lanes] = jnp.where(first, grad_a, grad_b)
        theirs[:, lanes] = jnp.where(first, grad_b, grad_a)

    sib = me_d + 1 - 2 * core
    sib_copy = remote(theirs, sib_recv, sib_sem.at[0], sib_sem.at[1], me_t, sib)
    sib_copy.start()
    sib_copy.wait()
    mine[...] = mine[...] + sib_recv[...]

    def along(axis, o):
        if axis == 0:
            at = (x + o) % AX
            return at * AX + z, me_d, at
        if axis == 1:
            at = (z + o) % AX
            return x * AX + at, me_d, at
        at = (y + o) % AX
        return me_t, at * 2 + core, at

    here = (x, z, y)
    orders = ((0, 1, 2), (1, 2, 0), (2, 0, 1))

    def step1_part(part, at):
        lanes = slice(part * PART, (part + 1) * PART)
        if part == 0:
            return mine[pl.ds(pl.multiple_of(at * 128, 128), 128), lanes].reshape(16, 8, PART)
        if part == 1:
            return jnp.concatenate(
                [
                    mine[pl.ds(pl.multiple_of(i * 128 + at * 32, 32), 32), lanes].reshape(4, 8, PART)
                    for i in range(4)
                ],
                axis=0,
            )
        return jnp.concatenate(
            [
                mine[pl.ds(pl.multiple_of(i * 32 + at * 8, 8), 8), lanes].reshape(1, 8, PART)
                for i in range(16)
            ],
            axis=0,
        )

    copies = []
    for o in (2, 1, 3):
        for part in range(3):
            tile, dp, at = along(orders[part][0], o)
            n = part * 3 + o - 1
            s1_send[n] = step1_part(part, at).reshape(128, PART).astype(BF16)
            copy = remote(s1_send.at[n], s1_recv.at[n], s1_ssem.at[n], s1_rsem.at[n], tile, dp)
            copy.start()
            copies.append(copy)
    for copy in copies:
        copy.wait()

    copies = []
    totals = []
    for part in range(3):
        total = step1_part(part, here[orders[part][0]])
        for o in range(3):
            total = total + s1_recv[part * 3 + o].astype(F32).reshape(16, 8, PART)
        s2_send[part] = total
    lead = (True, False, True)

    def step2_part(part, at):
        if lead[part]:
            return s2_send.at[part, pl.ds(at * 4, 4)]
        return s2_send.at[part, pl.ds(at, 4, stride=4)]

    for part in range(3):
        for o in (2, 1, 3):
            tile, dp, at = along(orders[part][1], o)
            n = part * 3 + o - 1
            if lead[part]:
                src = s2_send.at[part, pl.ds(at * 4, 4)]
            else:
                for i in range(4):
                    s3_send[n, i] = s2_send[part, i * 4 + at]
                src = s3_send.at[n]
            copy = remote(src, s2_recv.at[n], s2_ssem.at[n], s2_rsem.at[n], tile, dp)
            copy.start()
            copies.append(copy)
    for copy in copies:
        copy.wait()

    copies = []
    for part in range(3):
        at = here[orders[part][1]]
        if lead[part]:
            total = s2_send[part, pl.ds(at * 4, 4)]
        else:
            total = jnp.concatenate(
                [s2_send[part, pl.ds(i * 4 + at, 1)] for i in range(4)], axis=0
            )
        for o in range(3):
            total = total + s2_recv[part * 3 + o]
        fin_send[part] = total
        for o in (2, 1, 3):
            tile, dp, at = along(orders[part][2], o)
            n = part * 3 + o - 1
            copy = remote(
                fin_send.at[part, at], s3_recv.at[n], s3_ssem.at[n], s3_rsem.at[n], tile, dp
            )
            copy.start()
            copies.append(copy)
    for copy in copies:
        copy.wait()

    squares = jnp.zeros((8, C), F32)
    for part in range(3):
        total = fin_send[part, here[orders[part][2]]]
        for o in range(3):
            total = total + s3_recv[part * 3 + o]
        fin_recv[0, :, part * PART : (part + 1) * PART] = total
        for i in range(3):
            piece = total[:, i * C : (i + 1) * C]
            squares = squares + piece * piece
    fin_copy = remote(fin_recv.at[0], fin_recv.at[1], fin_sem.at[0], fin_sem.at[1], me_t, sib)
    fin_copy.start()

    nrm_send[...] = squares
    nrm_recv[0] = squares

    def n1_copy(o):
        return remote(nrm_send, nrm_recv.at[o], n1_ssem.at[o], n1_rsem.at[o], tile_peer(o), me_d)

    @pl.loop(1, N_TILE)
    def _(o):
        n1_copy(o).start()

    @pl.loop(1, N_TILE)
    def _(o):
        n1_copy(o).wait()

    plane = jnp.sum(nrm_recv[...], axis=0)
    nrm2_send[...] = plane
    nrm2_recv[me_d] = plane

    def n2_copy(o):
        return remote(
            nrm2_send, nrm2_recv.at[me_d], n2_ssem.at[o], n2_rsem.at[o], me_t, dp_peer(o)
        )

    @pl.loop(1, N_DP)
    def _(o):
        n2_copy(o).start()

    @pl.loop(1, N_DP)
    def _(o):
        n2_copy(o).wait()

    fin_copy.wait()
    total_a = jnp.sum(nrm2_recv[0] + nrm2_recv[2] + nrm2_recv[4] + nrm2_recv[6], keepdims=True)
    total_b = jnp.sum(nrm2_recv[1] + nrm2_recv[3] + nrm2_recv[5] + nrm2_recv[7], keepdims=True)
    root_a = jnp.sqrt(total_a / (HID * WIDE) + EPSILON)
    root_b = jnp.sqrt(total_b / (HID * WIDE) + EPSILON)
    first = core == 0
    full_a = jnp.where(first, fin_recv[0], fin_recv[1]) / root_a
    full_b = jnp.where(first, fin_recv[1], fin_recv[0]) / root_b
    upda_ref[...] = jnp.where(first, full_a[0:4], full_a[4:8])
    updb_ref[...] = jnp.where(first, full_b[0:4], full_b[4:8])


def local(*args):
    vmem = pl.BlockSpec(memory_space=pltpu.VMEM)
    smem = pl.BlockSpec(memory_space=pltpu.SMEM)
    hbm = pl.BlockSpec(memory_space=pl.ANY)
    dma = pltpu.SemaphoreType.DMA
    scratch = [
        pltpu.VMEM((64, 256, C), BF16),
        pltpu.VMEM((64, 256, C), F32),
        pltpu.VMEM((2, 64, C), F32),
        pltpu.VMEM((1, C), jnp.int32),
        pltpu.VMEM((N_TILE, 1, C), jnp.int32),
        pltpu.SMEM((N_TILE, 1, C), jnp.int32),
        pltpu.VMEM((N_TILE, 2, SIDE + 1, SIDE, C), BF16),
        pltpu.VMEM((N_TILE, 2, SIDE + 1, SIDE, C), BF16),
        pltpu.VMEM((NP, SIDE + 1, SIDE, C), BF16),
        pltpu.VMEM((NP, SIDE, C), F32),
        pltpu.VMEM((WIDE + C, HID), BF16),
        pltpu.VMEM((C, HID), F32),
        pltpu.VMEM((HID, WIDE), BF16),
        pltpu.VMEM((NP * SIDE, SIDE, WIDE + C), BF16),
        pltpu.VMEM((NP * SIDE, SIDE, WIDE), BF16),
        pltpu.VMEM((NP * CELLS, HID), BF16),
        pltpu.VMEM((NP * CELLS, HID), F32),
        pltpu.VMEM((NP * CELLS, HID), BF16),
        pltpu.VMEM((HID, WIDE), F32),
        pltpu.VMEM((HID, WIDE), F32),
        pltpu.VMEM((HID, WIDE), F32),
        pltpu.VMEM((9, 128, PART), BF16),
        pltpu.VMEM((9, 128, PART), BF16),
        pltpu.VMEM((3, 16, 8, PART), F32),
        pltpu.VMEM((9, 4, 8, PART), F32),
        pltpu.VMEM((9, 4, 8, PART), F32),
        pltpu.VMEM((9, 8, PART), F32),
        pltpu.VMEM((3, 4, 8, PART), F32),
        pltpu.VMEM((2, 8, WIDE), F32),
        pltpu.VMEM((8, C), F32),
        pltpu.VMEM((N_TILE, 8, C), F32),
        pltpu.VMEM((8, C), F32),
        pltpu.VMEM((N_DP, 8, C), F32),
        dma((3 + TAPS,)),
        dma((N_TILE,)),
        dma((N_TILE,)),
        dma((N_TILE,)),
        dma((N_TILE,)),
        dma((2,)),
        dma((9,)),
        dma((9,)),
        dma((9,)),
        dma((9,)),
        dma((9,)),
        dma((9,)),
        dma((2,)),
        dma((N_TILE,)),
        dma((N_TILE,)),
        dma((N_DP,)),
        dma((N_DP,)),
    ]
    return pl.pallas_call(
        kernel,
        out_shape=(
            jax.ShapeDtypeStruct((NP,), F32),
            jax.ShapeDtypeStruct((4, WIDE), F32),
            jax.ShapeDtypeStruct((4, WIDE), F32),
        ),
        in_specs=[hbm, vmem, smem, smem, smem, smem, smem, vmem, hbm, vmem, vmem, vmem, hbm, vmem, vmem],
        out_specs=(smem, vmem, vmem),
        scratch_shapes=scratch,
        compiler_params=pltpu.CompilerParams(
            collective_id=0, has_side_effects=True, vmem_limit_bytes=56 * 2**20
        ),
    )(*args)


def solution(mesh):
    both = ("tile", "dp")
    return jax.shard_map(
        local,
        mesh=mesh,
        in_specs=(
            P("tile", None, None),
            P("tile", None),
            P(both, None),
            P(both),
            P(both),
            P(both),
            P(both),
            P(both, None, None),
            P(),
            P(),
            P(),
            P(),
            P(),
            P(),
            P(),
        ),
        out_specs=(P(both), P(both, None), P(both, None)),
        check_vma=False,
    )
```

time: 629 us -> 89.1 us (0.14)
  local copies, waits for them, and re-layouts: 269 us -> 5.09 us
  waiting for transfers between devices: 177 us -> 0 us
  Pallas kernels: 0 us -> 83 us
  blocking collectives: 64.1 us -> 0 us
  matrix products: 44.8 us -> 0 us
  other arithmetic: 34.1 us -> 0 us
  starting transfers between devices: 18.7 us -> 0 us
  between operations: 16.5 us -> 0.64 us
    gather x194 -> x0, local copies, waits for them, and re-layouts: 191 us -> none
    unnamed x2 -> x0, waiting for transfers between devices: 158 us -> none
    pallas_call x0 -> x1, Pallas kernels: none -> 83 us  [local(): pl.pallas_call(kernel, out_shape=(jax.ShapeDtypeStruct((NP,), F32), jax.S...]
    psum x1 -> x0, blocking collectives: 64.1 us -> none  [local(): lax.psum((jnp.sum(shard_a * shard_a), jnp.sum(shard_b * shard_b)), ('tile...]
    scatter-add x7 -> x0, local copies, waits for them, and re-layouts: 58.4 us -> none  [patch_terms(): grad_hidden = grad_hidden.at[:, shift_row:shift_row + side_len, shift_col...]
    dot_general x46 -> x0, matrix products: 44.8 us -> none  [the longest x9 13.3 us: patch_terms(): lax.dot_general(grad_pre_b, w_b[tap_index * hidden_width:(tap_index + 1)...]
    all_to_all x3 -> x0, waiting for transfers between devices: 19.1 us -> none  [the longest x1 13.3 us: local(): lax.all_to_all(blocks, 'tile', split_axis=0, concat_axis=0, tiled=True)]
    all_to_all x3 -> x0, starting transfers between devices: 18.7 us -> none  [the longest x1 8.43 us: local(): lax.all_to_all(request_table, 'tile', split_axis=0, concat_axis=0, tiled=...]
  transfers between devices with their start and end apart: 4 -> 0, of which waited for: 3 -> 0; matrix products, arithmetic and copies ran while one was open for 19% -> 0% of each run, Pallas kernels for 0% -> 0%
where the time goes in v1:
time: 89.1 us; the launch traced here: 88.7 us
  Pallas kernels  83 us (93%)
  local copies, waits for them, and re-layouts  5.09 us (6%)
    pallas_call x1, Pallas kernels, local(): pl.pallas_call(kernel, out_shape=(jax.ShapeDtypeStruct((NP,), F32), jax.S...  83 us
    unnamed x4, local copies, waits for them, and re-layouts  5.09 us

profile of v1, /device:TPU:1, one launch (start us, length us, event | category | flops | bytes accessed | tf_op | source)
XLA Modules:
  0.0 88.7 jit_solution(3255397229566222553)
XLA Ops:
  0.6 1.3 %copy.18.owner_ref = s32[4,1]{1,0:T(4,128)} copy(s32[4,1]{0,1:T(1,128)} %param.17) | data formatting | bytes 32 | tf_op args[2]
  1.9 83.0 %shard_map.166 = (f32[4]{0:T(128)}, f32[4,1152]{1,0:T(4,128)}, f32[4,1152]{1,0:T(4,128)}) custom-call(bf16[64,256,128]{2,1,0:T(8,128)(2,1)} %feat_hbm.1, bf16[64,256]{1,0:T(8,128)(2,1)} %tgt_ref.1, s32[4,1]{1,0:T(4,128)} %copy.18.owner_ref, s32[4]{0:T(128)} %row_ref.1, s32[4]{0:T(128)} %col_ref.1, s32[4]{0:T(128)} %level_ref.1, s32[4]{0:T(128)} %count_ref.1, ...), custom_call_target="tpu_custom_call" | custom-call | tf_op jit(solution)/shard_map/pallas_call | solution.py:601
  85.0 1.1 %copy.22 = f32[4]{0:T(128)} copy(f32[4]{0:T(128)} %get-tuple-element.6) | data formatting | bytes 32
  86.1 1.3 %copy.23 = f32[4,1152]{1,0:T(4,128)} copy(f32[4,1152]{1,0:T(4,128)} %get-tuple-element.7) | data formatting | bytes 36864
  87.4 1.3 %copy.24 = f32[4,1152]{1,0:T(4,128)} copy(f32[4,1152]{1,0:T(4,128)} %get-tuple-element.8) | data formatting | bytes 36864

commit v2 on v1

v2 whole, which is shorter than its diff:
```python
import functools
import math

import jax
import jax.numpy as jnp
from jax import lax
from jax.experimental import pallas as pl
from jax.experimental.pallas import tpu as pltpu
from jax.sharding import PartitionSpec as P

C = 128
HID = 512
SIDE = 16
LEVELS = 32
NP = 4
CELLS = SIDE * SIDE
TAPS = 9
WIDE = TAPS * C
SIGMA_LOW = 0.02
SIGMA_HIGH = 80.0
SIGMA_DATA = 0.5
EPSILON = 1e-06
LOG_LOW = math.log(SIGMA_LOW)
LOG_STEP = (math.log(SIGMA_HIGH) - math.log(SIGMA_LOW)) / (LEVELS - 1)

MESH = pl.DeviceIdType.MESH
F32 = jnp.float32
BF16 = jnp.bfloat16
N_TILE = 16
N_DP = 8
AX = 4
PART = WIDE // 3


def iota(shape, dim):
    return lax.broadcasted_iota(jnp.int32, shape, dim)


def remote(src, dst, send_sem, recv_sem, tile, dp):
    return pltpu.make_async_remote_copy(
        src_ref=src,
        dst_ref=dst,
        send_sem=send_sem,
        recv_sem=recv_sem,
        device_id=(tile, dp),
        device_id_type=MESH,
    )


def column_shifts(block):
    col = iota(block.shape, 1)
    before = jnp.where(col == 0, 0.0, pltpu.roll(block, 1, axis=1))
    after = jnp.where(col == SIDE - 1, 0.0, pltpu.roll(block, SIDE - 1, axis=1))
    return before, block, after


def store_rows(dst, p, lane, rows, delta):
    lanes = slice(lane, lane + C)
    base = p * SIDE
    zero = jnp.zeros((1, SIDE, C), BF16)
    if delta == 0:
        dst[base : base + SIDE, :, lanes] = rows
    elif delta < 0:
        dst[base : base + 1, :, lanes] = zero
        dst[base + 1 : base + SIDE, :, lanes] = rows[: SIDE - 1]
    else:
        dst[base : base + SIDE - 1, :, lanes] = rows[1:]
        dst[base + SIDE - 1 : base + SIDE, :, lanes] = zero


def kernel(
    feat_hbm,
    tgt_hbm,
    owner_hbm,
    row_hbm,
    col_hbm,
    level_hbm,
    count_hbm,
    noise_hbm,
    wa_hbm,
    wu_hbm,
    ba_hbm,
    ea_hbm,
    wb_hbm,
    bb_hbm,
    wo_hbm,
    losses_ref,
    upda_ref,
    updb_ref,
    owner_ref,
    row_ref,
    col_ref,
    level_ref,
    count_ref,
    feat_v,
    feat_f,
    tgt_b,
    tgt_v,
    noise_b,
    noise_v,
    wu_ref,
    ba_ref,
    ea_ref,
    bb_ref,
    wo_ref,
    req_send,
    req_recv,
    req_smem,
    m1_send,
    m1_recv,
    m2_send,
    m2_recv0,
    m2_recv1,
    m2_recv2,
    m2_recv3,
    blk,
    wfull,
    wext,
    w2,
    left,
    right,
    slope,
    mine,
    sib_send,
    sib_recv,
    s1_send,
    s1_recv,
    tot2,
    s2_send,
    s2_recv,
    tot3,
    s3_recv,
    fin,
    nrm_send,
    nrm_recv,
    nrm2_send,
    nrm2_recv,
    local_sem,
    req_ssem,
    req_rsem,
    m1_ssem,
    m1_rsem,
    m2_ssem,
    m2_rsem,
    sib_ssem,
    sib_rsem,
    s1_ssem,
    s1_rsem,
    s2_ssem,
    s2_rsem,
    s3_ssem,
    s3_rsem,
    fin_sem,
    n1_ssem,
    n1_rsem,
    n2_ssem,
    n2_rsem,
):
    me_t = lax.axis_index("tile")
    me_d = lax.axis_index("dp")
    x, z = me_t >> 2, me_t & 3
    y, core = me_d >> 1, me_d & 1

    def tile_at(dx, dz):
        return (((x + dx) & 3) << 2) | ((z + dz) & 3)

    def tile_peer(o):
        return tile_at(o >> 2, o & 3)

    def dp_peer(o):
        return (me_d + o) & (N_DP - 1)

    m2_recv = (m2_recv0, m2_recv1, m2_recv2, m2_recv3)

    barrier = pltpu.get_barrier_semaphore()
    for o in range(1, N_TILE):
        pl.semaphore_signal(barrier, inc=1, device_id=(tile_peer(o), me_d), device_id_type=MESH)
    for o in range(1, N_DP):
        pl.semaphore_signal(barrier, inc=1, device_id=(me_t, dp_peer(o)), device_id_type=MESH)

    staged = []

    def stage(src, dst):
        copy = pltpu.make_async_copy(src, dst, local_sem.at[len(staged)])
        copy.start()
        staged.append(copy)
        return copy

    ints = [
        stage(a, b)
        for a, b in (
            (owner_hbm, owner_ref),
            (row_hbm, row_ref),
            (col_hbm, col_ref),
            (level_hbm, level_ref),
            (count_hbm, count_ref),
        )
    ]
    feat_copy = stage(feat_hbm, feat_v)
    tgt_copy = stage(tgt_hbm, tgt_b)
    small = [
        stage(a, b)
        for a, b in (
            (noise_hbm, noise_b),
            (wu_hbm, wu_ref),
            (ba_hbm, ba_ref),
            (ea_hbm, ea_ref),
            (bb_hbm, bb_ref),
            (wo_hbm, wo_ref),
        )
    ]
    small.append(stage(wa_hbm, wfull.at[pl.ds(0, WIDE)]))
    for t in range(TAPS):
        small.append(stage(wb_hbm.at[pl.ds(t * HID, HID)], w2.at[:, pl.ds(t * C, C)]))
    for copy in ints:
        copy.wait()

    lane = iota((1, C), 1)
    line = jnp.zeros((1, C), jnp.int32)
    for k in range(NP):
        line = jnp.where(lane == 4 * k, owner_ref[k], line)
        line = jnp.where(lane == 4 * k + 1, row_ref[k], line)
        line = jnp.where(lane == 4 * k + 2, col_ref[k], line)
    req_send[...] = line
    req_recv[me_t] = line
    pl.semaphore_wait(barrier, N_TILE - 1 + N_DP - 1)

    copies = []
    for o in range(1, N_TILE):
        copy = remote(
            req_send, req_recv.at[me_t], req_ssem.at[o], req_rsem.at[o], tile_peer(o), me_d
        )
        copy.start()
        copies.append(copy)

    tgt_copy.wait()
    tgt_v[0] = tgt_b[:, :C].astype(F32)
    tgt_v[1] = tgt_b[:, C:].astype(F32)
    feat_copy.wait()

    @pl.loop(0, 32)
    def _(i):
        feat_f[2 * i] = feat_v[2 * i].astype(F32)
        feat_f[2 * i + 1] = feat_v[2 * i + 1].astype(F32)

    for copy in copies:
        copy.wait()
    to_smem = pltpu.make_async_copy(req_recv, req_smem, local_sem.at[len(staged)])
    to_smem.start()
    to_smem.wait()

    lane2 = iota((SIDE, C), 1)

    def turn(value, shift):
        amount = jnp.full(value.shape, shift & (C - 1), jnp.int32)
        for bit in (1, 2, 4, 8, 16, 32, 64):
            value = jnp.where((amount & bit) != 0, pltpu.roll(value, bit, axis=1), value)
        return value

    def wanted(j):
        rank = jnp.int32(0)
        rows = [jnp.int32(0), jnp.int32(0)]
        cols = [jnp.int32(0), jnp.int32(0)]
        for k in range(NP):
            hit = req_smem[j, 0, 4 * k] == me_t
            for q in range(2):
                take = hit & (rank == q)
                rows[q] = jnp.where(take, req_smem[j, 0, 4 * k + 1], rows[q])
                cols[q] = jnp.where(take, req_smem[j, 0, 4 * k + 2], cols[q])
            rank = rank + hit.astype(jnp.int32)
        return rows, cols

    def fill(half, o, dst):
        def one(e, tile):
            rows, cols = wanted(tile_at(e, o) if half == 0 else tile_at(o, e))
            for q in range(2):
                block = feat_f[pl.ds(rows[q] + 8 * half, 8), pl.ds(cols[q], SIDE), :]
                dst[pl.ds((2 * e + q) * 8, 8)] = block.astype(BF16)
                if half == 0:
                    high = cols[q] >> 7
                    shift = cols[q] & (C - 1)
                    low_part = tgt_v[high, pl.ds(rows[q], SIDE), :]
                    next_part = tgt_v[1, pl.ds(rows[q], SIDE), :]
                    both = jnp.where(lane2 < shift, next_part, low_part)
                    both = turn(both, (2 * e + q) * SIDE - shift)
                    tile = jnp.where((lane2 >> 4) == 2 * e + q, both, tile)
            return tile

        tile = lax.fori_loop(0, AX, one, jnp.zeros((SIDE, C), F32))
        if half == 0:
            dst[64] = tile.astype(BF16)

    m1_copies = ([], [])
    for o in (2, 1, 3):
        for half in range(2):
            n = 3 * half + o - 1
            fill(half, o, m1_send.at[n])
            units = 65 - half
            copy = remote(
                m1_send.at[n, pl.ds(0, units)],
                m1_recv.at[half, o, pl.ds(0, units)],
                m1_ssem.at[n],
                m1_rsem.at[n],
                tile_at(0, o) if half == 0 else tile_at(o, 0),
                me_d,
            )
            copy.start()
            m1_copies[half].append(copy)
    for half in range(2):
        fill(half, 0, m1_recv.at[half, 0])

    for copy in small:
        copy.wait()
    wu = wu_ref[...]
    wu_hi = wu.astype(BF16).astype(F32)
    ba = ba_ref[...].reshape(1, HID)
    ba_hi = ba.astype(BF16).astype(F32)
    ea = ea_ref[...].reshape(1, HID)
    ea_hi = ea.astype(BF16).astype(F32)
    wext[...] = jnp.zeros_like(wext)
    wext[0:9] = wu_hi
    wext[9:18] = wu - wu_hi
    wext[18:27] = wu_hi
    wext[27:28] = ba_hi
    wext[28:29] = ba - ba_hi
    wext[29:30] = ea_hi
    wext[30:31] = ea - ea_hi
    wext[31:32] = ea_hi
    wfull[WIDE:, :] = wext[...].astype(BF16)
    noise_v[...] = jnp.zeros_like(noise_v)
    noise_v[:, :, 0:SIDE] = noise_b[...]

    for half in range(2):
        for copy in m1_copies[half]:
            copy.wait()

    def rank_of(j, k):
        rank = jnp.int32(0)
        for before in range(k):
            same = req_smem[j, 0, 4 * before] == req_smem[j, 0, 4 * k]
            rank = rank + same.astype(jnp.int32)
        return jnp.minimum(rank, 1)

    m2_copies = []
    for k in range(NP):
        row = []
        for e in (2, 1, 3, 0):
            for half in range(2):
                j = tile_at(e, 0) if half == 0 else tile_at(0, e)
                owner = req_smem[j, 0, 4 * k]
                rank = rank_of(j, k)
                if half == 0:
                    o = (z - (owner & 3)) & 3
                else:
                    o = (x - (owner >> 2)) & 3
                if e:
                    dst = m2_send.at[half * 4 + e, k]
                else:
                    dst = m2_recv[k].at[half, 0]
                dst[0:8] = m1_recv[half, o, pl.ds((2 * e + rank) * 8, 8)]
                if half == 0:
                    tile = m1_recv[0, o, 64].astype(F32)
                    if e:
                        tile = pltpu.roll(tile, C - 2 * e * SIDE, axis=1)
                    second = jnp.full(tile.shape, rank, jnp.int32) != 0
                    tile = jnp.where(second, pltpu.roll(tile, C - SIDE, axis=1), tile)
                    dst[8] = tile.astype(BF16)
                if e:
                    units = 9 - half
                    n = half * 16 + e * 4 + k
                    copy = remote(
                        m2_send.at[half * 4 + e, k, pl.ds(0, units)],
                        m2_recv[k].at[half, e, pl.ds(0, units)],
                        m2_ssem.at[n],
                        m2_rsem.at[n],
                        j,
                        me_d,
                    )
                    copy.start()
                    row.append(copy)
        m2_copies.append(row)

    wo = wo_ref[...].reshape(1, 1, C)
    bb = bb_ref[...].reshape(1, 1, C)
    shape3 = (SIDE, SIDE, C)
    col3, lane3 = iota(shape3, 1), iota(shape3, 2)
    none = jnp.zeros((1, SIDE, C), F32)
    for p in range(NP):
        for copy in m2_copies[p]:
            copy.wait()
        owner = owner_ref[p]
        from_x, from_z = (x - (owner >> 2)) & 3, (z - (owner & 3)) & 3
        blk[0:8] = m2_recv[p][0, from_x, 0:8]
        blk[8:16] = m2_recv[p][1, from_z, 0:8]
        clean = jnp.where(lane2 < SIDE, m2_recv[p][0, from_x, 8].astype(F32), 0.0)
        xcol = right.at[0]
        gcol = right.at[1]
        block = blk[...].astype(F32)
        for s, moved in enumerate(column_shifts(block)):
            rows = moved.astype(BF16)
            for r in range(3):
                store_rows(xcol, p, (3 * r + s) * C, rows, r - 1)

        level = jnp.full((SIDE, C), level_ref[p], jnp.int32).astype(F32)
        sigma = jnp.exp(LOG_LOW + level * LOG_STEP)
        variance = sigma * sigma + SIGMA_DATA * SIGMA_DATA
        scale_in = 1.0 / jnp.sqrt(variance)
        scale_skip = SIGMA_DATA * SIGMA_DATA / variance
        scale_out = sigma * SIGMA_DATA * scale_in
        embed = jnp.log(sigma) / 4.0
        noisy = clean + sigma * noise_v[p]
        aim = (clean - scale_skip * noisy) / scale_out
        scaled = pltpu.roll(scale_in * noisy, 1, axis=1)
        wide = jnp.broadcast_to(scaled[:, None, :], shape3)
        for bit in (1, 2, 4, 8):
            wide = jnp.where((col3 & bit) != 0, pltpu.roll(wide, C - bit, axis=2), wide)
        wide = jnp.where(lane3 < 3, wide, 0.0)
        taps = (
            jnp.concatenate([none, wide[: SIDE - 1]], axis=0)
            + pltpu.roll(wide, 3, axis=2)
            + pltpu.roll(jnp.concatenate([wide[1:], none], axis=0), 6, axis=2)
        )
        taps_hi = taps.astype(BF16).astype(F32)
        emb = embed[0:1, :][None]
        emb_hi = emb.astype(BF16).astype(F32)
        extra = taps_hi + pltpu.roll(taps_hi, 9, axis=2) + pltpu.roll(taps - taps_hi, 18, axis=2)
        extra = jnp.where((lane3 == 27) | (lane3 == 28), 1.0, extra)
        extra = jnp.where((lane3 == 29) | (lane3 == 30), emb_hi, extra)
        extra = jnp.where(lane3 == 31, emb - emb_hi, extra)
        xcol[p * SIDE : (p + 1) * SIDE, :, WIDE:] = extra.astype(BF16)

        cells = slice(p * CELLS, (p + 1) * CELLS)
        window = xcol[p * SIDE : (p + 1) * SIDE].reshape(CELLS, WIDE + C)
        pre_a = jnp.dot(window, wfull[...], preferred_element_type=F32)
        gate = jax.nn.sigmoid(pre_a)
        slope[...] = gate * (1.0 + pre_a * (1.0 - gate))
        hidden = (pre_a * gate).astype(BF16)
        left[1, cells] = hidden

        spread = jnp.dot(hidden, w2[...], preferred_element_type=F32).reshape(SIDE, SIDE, WIDE)

        def tap_rows(s):
            up = spread[:, :, s * C : (s + 1) * C]
            mid = spread[:, :, (3 + s) * C : (4 + s) * C]
            down = spread[:, :, (6 + s) * C : (7 + s) * C]
            return (
                mid
                + jnp.concatenate([none, up[: SIDE - 1]], axis=0)
                + jnp.concatenate([down[1:], none], axis=0)
            )

        before = jnp.where(col3 == 0, 0.0, pltpu.roll(tap_rows(0), 1, axis=1))
        after = jnp.where(col3 == SIDE - 1, 0.0, pltpu.roll(tap_rows(2), SIDE - 1, axis=1))
        pre_b = bb + tap_rows(1) + before + after
        gate_b = jax.nn.sigmoid(pre_b)
        aim3 = jnp.where(col3 == lane3, jnp.broadcast_to(aim[:, None, :], shape3), 0.0)
        residual = jnp.sum(pre_b * gate_b * wo - aim3, axis=2, keepdims=True)
        weight = count_ref[p].astype(F32)
        losses_ref[p] = jnp.sum(residual * residual) * weight / CELLS
        grad_final = (2.0 * weight / CELLS) * residual
        grad_b = grad_final * wo * (gate_b * (1.0 + pre_b * (1.0 - gate_b)))
        grad_b = grad_b.astype(BF16).astype(F32)
        for s, moved in enumerate(column_shifts(grad_b)):
            rows = moved.astype(BF16)
            for r in range(3):
                store_rows(gcol, p, (3 * (2 - r) + (2 - s)) * C, rows, r - 1)

        back = lax.dot_general(
            gcol[p * SIDE : (p + 1) * SIDE, :, 0:WIDE].reshape(CELLS, WIDE),
            w2[...],
            (((1,), (1,)), ((), ())),
            preferred_element_type=F32,
        )
        left[0, cells] = (back * slope[...]).astype(BF16)

    sib = me_d ^ 1

    def gradient(which, part):
        return lax.dot_general(
            left[which],
            right[which, :, :, part * PART : (part + 1) * PART].reshape(NP * CELLS, PART),
            (((0,), (0,)), ((), ())),
            preferred_element_type=F32,
        )

    def along(axis, o):
        if axis == 0:
            at = (x + o) & 3
            return (at << 2) | z, me_d, at
        if axis == 1:
            at = (z + o) & 3
            return (x << 2) | at, me_d, at
        at = (y + o) & 3
        return me_t, (at << 1) | core, at

    here = (x, z, y)
    orders = ((0, 1, 2), (1, 2, 0), (2, 0, 1))
    full = (AX, AX, 8, PART)

    def piece1(part, at):
        if part == 0:
            return mine[part, at]
        if part == 1:
            return mine[part, :, at]
        return mine[part, :, :, at]

    s1_copies = []

    def step1(part):
        sib_copies[part].wait()
        mine[part] = mine[part] + sib_recv[part].astype(F32).reshape(AX, AX, AX, 8, PART)
        row = []
        for o in (2, 1, 3):
            tile, dp, at = along(orders[part][0], o)
            n = part * 3 + o - 1
            s1_send[n] = piece1(part, at).reshape(128, PART).astype(BF16)
            copy = remote(s1_send.at[n], s1_recv.at[n], s1_ssem.at[n], s1_rsem.at[n], tile, dp)
            copy.start()
            row.append(copy)
        s1_copies.append(row)

    sib_copies = []
    for part in range(3):
        sib_send[part] = gradient(1 - core, part).astype(BF16)
        copy = remote(
            sib_send.at[part], sib_recv.at[part], sib_ssem.at[part], sib_rsem.at[part], me_t, sib
        )
        copy.start()
        sib_copies.append(copy)
        mine[part] = gradient(core, part).reshape(AX, AX, AX, 8, PART)
        if part:
            step1(part - 1)
    step1(2)

    def piece2(part, at):
        return tot2[part, :, at] if part == 1 else tot2[part, at]

    s2_copies = []
    for part in range(3):
        for copy in s1_copies[part]:
            copy.wait()
        total = piece1(part, here[orders[part][0]])
        for o in range(3):
            total = total + s1_recv[part * 3 + o].astype(F32).reshape(full)
        tot2[part] = total
        row = []
        for o in (2, 1, 3):
            tile, dp, at = along(orders[part][1], o)
            n = part * 3 + o - 1
            s2_send[n] = piece2(part, at).reshape(32, PART).astype(BF16)
            copy = remote(s2_send.at[n], s2_recv.at[n], s2_ssem.at[n], s2_rsem.at[n], tile, dp)
            copy.start()
            row.append(copy)
        s2_copies.append(row)

    s3_copies = []
    for part in range(3):
        for copy in s2_copies[part]:
            copy.wait()
        total = piece2(part, here[orders[part][1]])
        for o in range(3):
            total = total + s2_recv[part * 3 + o].astype(F32).reshape(AX, 8, PART)
        tot3[part] = total
        row = []
        for o in (2, 1, 3):
            tile, dp, at = along(orders[part][2], o)
            n = part * 3 + o - 1
            copy = remote(
                tot3.at[part, at], s3_recv.at[n], s3_ssem.at[n], s3_rsem.at[n], tile, dp
            )
            copy.start()
            row.append(copy)
        s3_copies.append(row)

    squares = jnp.zeros((8, C), F32)
    for part in range(3):
        for copy in s3_copies[part]:
            copy.wait()
        total = tot3[part, here[orders[part][2]]]
        for o in range(3):
            total = total + s3_recv[part * 3 + o]
        fin[0, :, part * PART : (part + 1) * PART] = total
        for i in range(3):
            piece = total[:, i * C : (i + 1) * C]
            squares = squares + piece * piece

    nrm_send[...] = squares
    nrm_recv[0] = squares
    copies = []
    for o in range(1, N_TILE):
        copy = remote(nrm_send, nrm_recv.at[o], n1_ssem.at[o], n1_rsem.at[o], tile_peer(o), me_d)
        copy.start()
        copies.append(copy)
    fin_copy = remote(fin.at[0], fin.at[1], fin_sem.at[0], fin_sem.at[1], me_t, sib)
    fin_copy.start()
    for copy in copies:
        copy.wait()
    plane = jnp.sum(nrm_recv[...], axis=0)
    nrm2_send[...] = plane
    nrm2_recv[me_d] = plane
    copies = []
    for o in range(1, N_DP):
        copy = remote(
            nrm2_send, nrm2_recv.at[me_d], n2_ssem.at[o], n2_rsem.at[o], me_t, dp_peer(o)
        )
        copy.start()
        copies.append(copy)
    fin_copy.wait()
    for copy in copies:
        copy.wait()

    total_a = jnp.sum(nrm2_recv[0] + nrm2_recv[2] + nrm2_recv[4] + nrm2_recv[6], keepdims=True)
    total_b = jnp.sum(nrm2_recv[1] + nrm2_recv[3] + nrm2_recv[5] + nrm2_recv[7], keepdims=True)
    root_a = jnp.sqrt(total_a / (HID * WIDE) + EPSILON)
    root_b = jnp.sqrt(total_b / (HID * WIDE) + EPSILON)
    full_a = fin[core] / root_a
    full_b = fin[1 - core] / root_b
    first = core == 0
    upda_ref[...] = jnp.where(first, full_a[0:4], full_a[4:8])
    updb_ref[...] = jnp.where(first, full_b[0:4], full_b[4:8])


def leave(a_in, b_in, c_in, a_out, b_out, c_out, sem):
    pairs = ((a_in, a_out), (b_in, b_out), (c_in, c_out))
    copies = [pltpu.make_async_copy(s, d, sem.at[i]) for i, (s, d) in enumerate(pairs)]
    for copy in copies:
        copy.start()
    for copy in copies:
        copy.wait()


def local(features, target_field, owner_tile, *rest):
    vmem = pl.BlockSpec(memory_space=pltpu.VMEM)
    smem = pl.BlockSpec(memory_space=pltpu.SMEM)
    hbm = pl.BlockSpec(memory_space=pl.ANY)
    dma = pltpu.SemaphoreType.DMA
    ints = pltpu.SMEM((NP,), jnp.int32)
    scratch = [
        ints,
        ints,
        ints,
        ints,
        ints,
        pltpu.VMEM((64, 256, C), BF16),
        pltpu.VMEM((64, 256, C), F32),
        pltpu.VMEM((64, 256), BF16),
        pltpu.VMEM((2, 64, C), F32),
        pltpu.VMEM((NP, SIDE, SIDE), F32),
        pltpu.VMEM((NP, SIDE, C), F32),
        pltpu.VMEM((TAPS, HID), F32),
        pltpu.VMEM((HID,), F32),
        pltpu.VMEM((HID,), F32),
        pltpu.VMEM((C,), F32),
        pltpu.VMEM((C,), F32),
        pltpu.VMEM((1, C), jnp.int32),
        pltpu.VMEM((N_TILE, 1, C), jnp.int32),
        pltpu.SMEM((N_TILE, 1, C), jnp.int32),
        pltpu.VMEM((6, 65, SIDE, C), BF16),
        pltpu.VMEM((2, AX, 65, SIDE, C), BF16),
        pltpu.VMEM((8, NP, 9, SIDE, C), BF16),
        pltpu.VMEM((2, AX, 9, SIDE, C), BF16),
        pltpu.VMEM((2, AX, 9, SIDE, C), BF16),
        pltpu.VMEM((2, AX, 9, SIDE, C), BF16),
        pltpu.VMEM((2, AX, 9, SIDE, C), BF16),
        pltpu.VMEM((SIDE, SIDE, C), BF16),
        pltpu.VMEM((WIDE + C, HID), BF16),
        pltpu.VMEM((C, HID), F32),
        pltpu.VMEM((HID, WIDE), BF16),
        pltpu.VMEM((2, NP * CELLS, HID), BF16),
        pltpu.VMEM((2, NP * SIDE, SIDE, WIDE + C), BF16),
        pltpu.VMEM((CELLS, HID), F32),
        pltpu.VMEM((3, AX, AX, AX, 8, PART), F32),
        pltpu.VMEM((3, HID, PART), BF16),
        pltpu.VMEM((3, HID, PART), BF16),
        pltpu.VMEM((9, 128, PART), BF16),
        pltpu.VMEM((9, 128, PART), BF16),
        pltpu.VMEM((3, AX, AX, 8, PART), F32),
        pltpu.VMEM((9, 32, PART), BF16),
        pltpu.VMEM((9, 32, PART), BF16),
        pltpu.VMEM((3, AX, 8, PART), F32),
        pltpu.VMEM((9, 8, PART), F32),
        pltpu.VMEM((2, 8, WIDE), F32),
        pltpu.VMEM((8, C), F32),
        pltpu.VMEM((N_TILE, 8, C), F32),
        pltpu.VMEM((8, C), F32),
        pltpu.VMEM((N_DP, 8, C), F32),
        dma((32,)),
        dma((N_TILE,)),
        dma((N_TILE,)),
        dma((6,)),
        dma((6,)),
        dma((32,)),
        dma((32,)),
        dma((3,)),
        dma((3,)),
        dma((9,)),
        dma((9,)),
        dma((9,)),
        dma((9,)),
        dma((9,)),
        dma((9,)),
        dma((2,)),
        dma((N_TILE,)),
        dma((N_TILE,)),
        dma((N_DP,)),
        dma((N_DP,)),
    ]
    outs = (
        jax.ShapeDtypeStruct((NP,), F32),
        jax.ShapeDtypeStruct((4, WIDE), F32),
        jax.ShapeDtypeStruct((4, WIDE), F32),
    )
    results = pl.pallas_call(
        kernel,
        out_shape=outs,
        in_specs=[hbm] * 15,
        out_specs=(smem, vmem, vmem),
        scratch_shapes=scratch,
        compiler_params=pltpu.CompilerParams(
            collective_id=0, has_side_effects=True, vmem_limit_bytes=60 * 2**20
        ),
    )(features, target_field, owner_tile.reshape(-1), *rest)
    return pl.pallas_call(
        leave,
        out_shape=outs,
        in_specs=[hbm] * 3,
        out_specs=(hbm,) * 3,
        scratch_shapes=[dma((3,))],
    )(*results)


def solution(mesh):
    both = ("tile", "dp")
    return jax.shard_map(
        local,
        mesh=mesh,
        in_specs=(
            P("tile", None, None),
            P("tile", None),
            P(both, None),
            P(both),
            P(both),
            P(both),
            P(both),
            P(both, None, None),
            P(),
            P(),
            P(),
            P(),
            P(),
            P(),
            P(),
        ),
        out_specs=(P(both), P(both, None), P(both, None)),
        check_vma=False,
    )
```

time: 89.1 us -> 75.2 us (0.84)
  Pallas kernels: 83 us -> 74.4 us
  local copies, waits for them, and re-layouts: 5.09 us -> 0 us
    pallas_call x1 -> x2, Pallas kernels: 83 us -> 74.4 us  [the longest x1 72.1 us: local(): pl.pallas_call(kernel, out_shape=outs, in_specs=[hbm] * 15, out_specs=(sm...]
    unnamed x4 -> x0, local copies, waits for them, and re-layouts: 5.09 us -> none
where the time goes in v2:
time: 75.2 us; the launch traced here: 75.1 us
  Pallas kernels  74.4 us (99%)
    pallas_call x1, Pallas kernels, local(): pl.pallas_call(kernel, out_shape=outs, in_specs=[hbm] * 15, out_specs=(sm...  72.1 us
    pallas_call x1, Pallas kernels, local(): pl.pallas_call(leave, out_shape=outs, in_specs=[hbm] * 3, out_specs=(hbm,...  2.26 us

profile of v2, /device:TPU:1, one launch (start us, length us, event | category | flops | bytes accessed | tf_op | source)
XLA Modules:
  0.0 75.1 jit_solution(1593243464989057492)
XLA Ops:
  0.6 72.1 %shard_map.166 = (f32[4]{0:T(128)}, f32[4,1152]{1,0:T(4,128)}, f32[4,1152]{1,0:T(4,128)}) custom-call(bf16[64,256,128]{2,1,0:T(8,128)(2,1)} %feat_hbm.1, bf16[64,256]{1,0:T(8,128)(2,1)} %tgt_hbm.1, s32[4]{0:T(128)} %bitcast.1, s32[4]{0:T(128)} %row_hbm.1, s32[4]{0:T(128)} %col_hbm.1, s32[4]{0:T(128)} %level_hbm.1, s32[4]{0:T(128)} %count_hbm.1, ...), custom_call_target="tpu_custom_call" | custom-call | tf_op jit(solution)/shard_map/pallas_call | solution.py:713
  72.8 2.3 %shard_map.167 = (f32[4]{0:T(128)}, f32[4,1152]{1,0:T(4,128)}, f32[4,1152]{1,0:T(4,128)}) custom-call(f32[4]{0:T(128)} %get-tuple-element.6.a_in, f32[4,1152]{1,0:T(4,128)} %get-tuple-element.7.b_in, f32[4,1152]{1,0:T(4,128)} %get-tuple-element.8.c_in), custom_call_target="tpu_custom_call" | custom-call | tf_op jit(solution)/shard_map/pallas_call | solution.py:723

commit v3 on v2

--- a/solution.py
+++ b/solution.py
@@ -121,8 +121,6 @@
     right,
     slope,
     mine,
-    sib_send,
-    sib_recv,
     s1_send,
     s1_recv,
     tot2,
@@ -173,11 +171,6 @@
     m2_recv = (m2_recv0, m2_recv1, m2_recv2, m2_recv3)
 
     barrier = pltpu.get_barrier_semaphore()
-    for o in range(1, N_TILE):
-        pl.semaphore_signal(barrier, inc=1, device_id=(tile_peer(o), me_d), device_id_type=MESH)
-    for o in range(1, N_DP):
-        pl.semaphore_signal(barrier, inc=1, device_id=(me_t, dp_peer(o)), device_id_type=MESH)
-
     staged = []
 
     def stage(src, dst):
@@ -196,6 +189,11 @@
             (count_hbm, count_ref),
         )
     ]
+    for o in range(1, N_TILE):
+        pl.semaphore_signal(barrier, inc=1, device_id=(tile_peer(o), me_d), device_id_type=MESH)
+    for o in range(1, N_DP):
+        pl.semaphore_signal(barrier, inc=1, device_id=(me_t, dp_peer(o)), device_id_type=MESH)
+
     feat_copy = stage(feat_hbm, feat_v)
     tgt_copy = stage(tgt_hbm, tgt_b)
     small = [
@@ -286,7 +284,7 @@
                     tile = jnp.where((lane2 >> 4) == 2 * e + q, both, tile)
             return tile
 
-        tile = lax.fori_loop(0, AX, one, jnp.zeros((SIDE, C), F32))
+        tile = lax.fori_loop(0, AX, one, jnp.zeros((SIDE, C), F32), unroll=True)
         if half == 0:
             dst[64] = tile.astype(BF16)
 
@@ -380,6 +378,8 @@
                     row.append(copy)
         m2_copies.append(row)
 
+    sib = me_d ^ 1
+    pair_copies = []
     wo = wo_ref[...].reshape(1, 1, C)
     bb = bb_ref[...].reshape(1, 1, C)
     shape3 = (SIDE, SIDE, C)
@@ -473,12 +473,36 @@
         )
         left[0, cells] = (back * slope[...]).astype(BF16)
 
-    sib = me_d ^ 1
-
-    def gradient(which, part):
+        row = []
+        for i, ref in enumerate((left, right)):
+            size = CELLS if i == 0 else SIDE
+            lanes = pl.ds(0, HID if i == 0 else WIDE)
+            middle = () if i == 0 else (slice(None),)
+            copy = remote(
+                ref.at[(1 - core, pl.ds(p * size, size)) + middle + (lanes,)],
+                ref.at[(1 - core, pl.ds((NP + p) * size, size)) + middle + (lanes,)],
+                sib_ssem.at[2 * p + i],
+                sib_rsem.at[2 * p + i],
+                me_t,
+                sib,
+            )
+            copy.start()
+            row.append(copy)
+        pair_copies.append(row)
+
+    for row in pair_copies[: NP - 1]:
+        for copy in row:
+            copy.wait()
+
+    def gradient(chunk, first, count):
         return lax.dot_general(
-            left[which],
-            right[which, :, :, part * PART : (part + 1) * PART].reshape(NP * CELLS, PART),
+            left[core, first * CELLS : (first + count) * CELLS],
+            right[
+                core,
+                first * SIDE : (first + count) * SIDE,
+                :,
+                chunk * PART : (chunk + 1) * PART,
+            ].reshape(count * CELLS, PART),
             (((0,), (0,)), ((), ())),
             preferred_element_type=F32,
         )
@@ -495,42 +519,39 @@
 
     here = (x, z, y)
     orders = ((0, 1, 2), (1, 2, 0), (2, 0, 1))
-    full = (AX, AX, 8, PART)
-
-    def piece1(part, at):
+
+    def piece1(chunk, part, at):
+        lanes = slice(part * C, (part + 1) * C)
         if part == 0:
-            return mine[part, at]
+            return mine[chunk, at, :, :, :, lanes]
         if part == 1:
-            return mine[part, :, at]
-        return mine[part, :, :, at]
-
-    s1_copies = []
-
-    def step1(part):
-        sib_copies[part].wait()
-        mine[part] = mine[part] + sib_recv[part].astype(F32).reshape(AX, AX, AX, 8, PART)
-        row = []
+            return mine[chunk, :, at, :, :, lanes]
+        return mine[chunk, :, :, at, :, lanes]
+
+    s1_copies = [[], [], []]
+
+    def step1(chunk):
+        if chunk == 0:
+            total = gradient(chunk, 0, 2 * NP - 1)
+            for copy in pair_copies[NP - 1]:
+                copy.wait()
+            total = total + gradient(chunk, 2 * NP - 1, 1)
+        else:
+            total = gradient(chunk, 0, 2 * NP)
+        mine[chunk] = total.reshape(AX, AX, AX, 8, PART)
         for o in (2, 1, 3):
-            tile, dp, at = along(orders[part][0], o)
-            n = part * 3 + o - 1
-            s1_send[n] = piece1(part, at).reshape(128, PART).astype(BF16)
-            copy = remote(s1_send.at[n], s1_recv.at[n], s1_ssem.at[n], s1_rsem.at[n], tile, dp)
-            copy.start()
-            row.append(copy)
-        s1_copies.append(row)
-
-    sib_copies = []
-    for part in range(3):
-        sib_send[part] = gradient(1 - core, part).astype(BF16)
-        copy = remote(
-            sib_send.at[part], sib_recv.at[part], sib_ssem.at[part], sib_rsem.at[part], me_t, sib
-        )
-        copy.start()
-        sib_copies.append(copy)
-        mine[part] = gradient(core, part).reshape(AX, AX, AX, 8, PART)
-        if part:
-            step1(part - 1)
-    step1(2)
+            for part in range(3):
+                tile, dp, at = along(orders[part][0], o)
+                n = chunk * 9 + part * 3 + o - 1
+                s1_send[n] = piece1(chunk, part, at).reshape(128, C).astype(BF16)
+                copy = remote(
+                    s1_send.at[n], s1_recv.at[n], s1_ssem.at[n], s1_rsem.at[n], tile, dp
+                )
+                copy.start()
+                s1_copies[part].append(copy)
+
+    for chunk in range(3):
+        step1(chunk)
 
     def piece2(part, at):
         return tot2[part, :, at] if part == 1 else tot2[part, at]
@@ -539,10 +560,12 @@
     for part in range(3):
         for copy in s1_copies[part]:
             copy.wait()
-        total = piece1(part, here[orders[part][0]])
-        for o in range(3):
-            total = total + s1_recv[part * 3 + o].astype(F32).reshape(full)
-        tot2[part] = total
+        for chunk in range(3):
+            total = piece1(chunk, part, here[orders[part][0]])
+            for o in range(3):
+                landed = s1_recv[chunk * 9 + part * 3 + o].astype(F32)
+                total = total + landed.reshape(AX, AX, 8, C)
+            tot2[part, :, :, :, chunk * C : (chunk + 1) * C] = total
         row = []
         for o in (2, 1, 3):
             tile, dp, at = along(orders[part][1], o)
@@ -579,9 +602,9 @@
         total = tot3[part, here[orders[part][2]]]
         for o in range(3):
             total = total + s3_recv[part * 3 + o]
-        fin[0, :, part * PART : (part + 1) * PART] = total
         for i in range(3):
             piece = total[:, i * C : (i + 1) * C]
+            fin[0, :, (3 * i + part) * C : (3 * i + part + 1) * C] = piece
             squares = squares + piece * piece
 
     nrm_send[...] = squares
@@ -666,14 +689,12 @@
         pltpu.VMEM((WIDE + C, HID), BF16),
         pltpu.VMEM((C, HID), F32),
         pltpu.VMEM((HID, WIDE), BF16),
-        pltpu.VMEM((2, NP * CELLS, HID), BF16),
-        pltpu.VMEM((2, NP * SIDE, SIDE, WIDE + C), BF16),
+        pltpu.VMEM((2, 2 * NP * CELLS, HID), BF16),
+        pltpu.VMEM((2, 2 * NP * SIDE, SIDE, WIDE + C), BF16),
         pltpu.VMEM((CELLS, HID), F32),
         pltpu.VMEM((3, AX, AX, AX, 8, PART), F32),
-        pltpu.VMEM((3, HID, PART), BF16),
-        pltpu.VMEM((3, HID, PART), BF16),
-        pltpu.VMEM((9, 128, PART), BF16),
-        pltpu.VMEM((9, 128, PART), BF16),
+        pltpu.VMEM((27, 128, C), BF16),
+        pltpu.VMEM((27, 128, C), BF16),
         pltpu.VMEM((3, AX, AX, 8, PART), F32),
         pltpu.VMEM((9, 32, PART), BF16),
         pltpu.VMEM((9, 32, PART), BF16),
@@ -691,10 +712,10 @@
         dma((6,)),
         dma((32,)),
         dma((32,)),
-        dma((3,)),
-        dma((3,)),
-        dma((9,)),
-        dma((9,)),
+        dma((2 * NP,)),
+        dma((2 * NP,)),
+        dma((27,)),
+        dma((27,)),
         dma((9,)),
         dma((9,)),
         dma((9,)),

time: 75.2 us -> 72.3 us (0.961)
  Pallas kernels: 74.4 us -> 71.5 us
    pallas_call x1, Pallas kernels: 72.1 us -> 69.3 us  [local(): pl.pallas_call(kernel, out_shape=outs, in_specs=[hbm] * 15, out_specs=(sm...]
where the time goes in v3:
time: 72.3 us; the launch traced here: 72.2 us
  Pallas kernels  71.5 us (99%)
    pallas_call x1, Pallas kernels, local(): pl.pallas_call(kernel, out_shape=outs, in_specs=[hbm] * 15, out_specs=(sm...  69.3 us
    pallas_call x1, Pallas kernels, local(): pl.pallas_call(leave, out_shape=outs, in_specs=[hbm] * 3, out_specs=(hbm,...  2.26 us

profile of v3, /device:TPU:1, one launch (start us, length us, event | category | flops | bytes accessed | tf_op | source)
XLA Modules:
  0.0 72.2 jit_solution(3705764270558870078)
XLA Ops:
  0.6 69.3 %shard_map.166 = (f32[4]{0:T(128)}, f32[4,1152]{1,0:T(4,128)}, f32[4,1152]{1,0:T(4,128)}) custom-call(bf16[64,256,128]{2,1,0:T(8,128)(2,1)} %feat_hbm.1, bf16[64,256]{1,0:T(8,128)(2,1)} %tgt_hbm.1, s32[4]{0:T(128)} %bitcast.1, s32[4]{0:T(128)} %row_hbm.1, s32[4]{0:T(128)} %col_hbm.1, s32[4]{0:T(128)} %level_hbm.1, s32[4]{0:T(128)} %count_hbm.1, ...), custom_call_target="tpu_custom_call" | custom-call | tf_op jit(solution)/shard_map/pallas_call | solution.py:734
  69.9 2.3 %shard_map.167 = (f32[4]{0:T(128)}, f32[4,1152]{1,0:T(4,128)}, f32[4,1152]{1,0:T(4,128)}) custom-call(f32[4]{0:T(128)} %get-tuple-element.6.a_in, f32[4,1152]{1,0:T(4,128)} %get-tuple-element.7.b_in, f32[4,1152]{1,0:T(4,128)} %get-tuple-element.8.c_in), custom_call_target="tpu_custom_call" | custom-call | tf_op jit(solution)/shard_map/pallas_call | solution.py:744

commit v4 on v3

--- a/solution.py
+++ b/solution.py
@@ -55,7 +55,7 @@
 
 
 def store_rows(dst, p, lane, rows, delta):
-    lanes = slice(lane, lane + C)
+    lanes = pl.ds(lane, C)
     base = p * SIDE
     zero = jnp.zeros((1, SIDE, C), BF16)
     if delta == 0:
@@ -120,6 +120,8 @@
     left,
     right,
     slope,
+    raw_send,
+    raw_recv,
     mine,
     s1_send,
     s1_recv,
@@ -460,6 +462,7 @@
         grad_final = (2.0 * weight / CELLS) * residual
         grad_b = grad_final * wo * (gate_b * (1.0 + pre_b * (1.0 - gate_b)))
         grad_b = grad_b.astype(BF16).astype(F32)
+        raw_send[p] = jnp.where(core == 0, grad_b, block).astype(BF16)
         for s, moved in enumerate(column_shifts(grad_b)):
             rows = moved.astype(BF16)
             for r in range(3):
@@ -474,25 +477,34 @@
         left[0, cells] = (back * slope[...]).astype(BF16)
 
         row = []
-        for i, ref in enumerate((left, right)):
-            size = CELLS if i == 0 else SIDE
-            lanes = pl.ds(0, HID if i == 0 else WIDE)
-            middle = () if i == 0 else (slice(None),)
+        for i, src, dst in (
+            (0, raw_send.at[p], raw_recv.at[p]),
+            (
+                1,
+                left.at[1 - core, pl.ds(p * CELLS, CELLS)],
+                left.at[1 - core, pl.ds((NP + p) * CELLS, CELLS)],
+            ),
+        ):
             copy = remote(
-                ref.at[(1 - core, pl.ds(p * size, size)) + middle + (lanes,)],
-                ref.at[(1 - core, pl.ds((NP + p) * size, size)) + middle + (lanes,)],
-                sib_ssem.at[2 * p + i],
-                sib_rsem.at[2 * p + i],
-                me_t,
-                sib,
+                src, dst, sib_ssem.at[2 * p + i], sib_rsem.at[2 * p + i], me_t, sib
             )
             copy.start()
             row.append(copy)
         pair_copies.append(row)
 
-    for row in pair_copies[: NP - 1]:
-        for copy in row:
+    def sibling_columns(p):
+        for copy in pair_copies[p]:
             copy.wait()
+        dst = right.at[core]
+        for s, moved in enumerate(column_shifts(raw_recv[p].astype(F32))):
+            rows = moved.astype(BF16)
+            for r in range(3):
+                tap = 3 * r + s
+                lane = pl.multiple_of(jnp.where(core == 0, tap, TAPS - 1 - tap) * C, C)
+                store_rows(dst, NP + p, lane, rows, r - 1)
+
+    for p in range(NP - 1):
+        sibling_columns(p)
 
     def gradient(chunk, first, count):
         return lax.dot_general(
@@ -533,8 +545,7 @@
     def step1(chunk):
         if chunk == 0:
             total = gradient(chunk, 0, 2 * NP - 1)
-            for copy in pair_copies[NP - 1]:
-                copy.wait()
+            sibling_columns(NP - 1)
             total = total + gradient(chunk, 2 * NP - 1, 1)
         else:
             total = gradient(chunk, 0, 2 * NP)
@@ -692,6 +703,8 @@
         pltpu.VMEM((2, 2 * NP * CELLS, HID), BF16),
         pltpu.VMEM((2, 2 * NP * SIDE, SIDE, WIDE + C), BF16),
         pltpu.VMEM((CELLS, HID), F32),
+        pltpu.VMEM((NP, SIDE, SIDE, C), BF16),
+        pltpu.VMEM((NP, SIDE, SIDE, C), BF16),
         pltpu.VMEM((3, AX, AX, AX, 8, PART), F32),
         pltpu.VMEM((27, 128, C), BF16),
         pltpu.VMEM((27, 128, C), BF16),
@@ -733,7 +746,7 @@
     )
     results = pl.pallas_call(
         kernel,
-        out_shape=outs,
+        out_shape=(outs[0], pltpu.VMEM((4, WIDE), F32), pltpu.VMEM((4, WIDE), F32)),
         in_specs=[hbm] * 15,
         out_specs=(smem, vmem, vmem),
         scratch_shapes=scratch,
@@ -744,10 +757,10 @@
     return pl.pallas_call(
         leave,
         out_shape=outs,
-        in_specs=[hbm] * 3,
+        in_specs=[hbm, vmem, vmem],
         out_specs=(hbm,) * 3,
         scratch_shapes=[dma((3,))],
-    )(*results)
+    )(results[0], *[pltpu.with_memory_space_constraint(a, pltpu.VMEM) for a in results[1:]])
 
 
 def solution(mesh):

time: 72.3 us -> 70.3 us (0.972)
  Pallas kernels: 71.5 us -> 69.5 us
    pallas_call x2, Pallas kernels: 71.5 us -> 69.5 us  [the longest x1 68.4 us: local(): pl.pallas_call(kernel, out_shape=(outs[0], pltpu.VMEM((4, WIDE), F32), pl...]
where the time goes in v4:
time: 70.3 us; the launch traced here: 70.2 us
  Pallas kernels  69.5 us (99%)
    pallas_call x1, Pallas kernels, local(): pl.pallas_call(kernel, out_shape=(outs[0], pltpu.VMEM((4, WIDE), F32), pl...  68.4 us

profile of v4, /device:TPU:1, one launch (start us, length us, event | category | flops | bytes accessed | tf_op | source)
XLA Modules:
  0.0 70.2 jit_solution(13706457405893701049)
XLA Ops:
  0.6 68.4 %shard_map.166 = (f32[4]{0:T(128)}, f32[4,1152]{1,0:T(4,128)S(1)}, f32[4,1152]{1,0:T(4,128)S(1)}) custom-call(bf16[64,256,128]{2,1,0:T(8,128)(2,1)} %feat_hbm.1, bf16[64,256]{1,0:T(8,128)(2,1)} %tgt_hbm.1, s32[4]{0:T(128)} %bitcast.1, s32[4]{0:T(128)} %row_hbm.1, s32[4]{0:T(128)} %col_hbm.1, s32[4]{0:T(128)} %level_hbm.1, s32[4]{0:T(128)} %count_hbm.1, ...), custom_call_target="tpu_custom_call" | custom-call | tf_op jit(solution)/shard_map/pallas_call | solution.py:747
  69.0 1.1 %shard_map.167 = (f32[4]{0:T(128)}, f32[4,1152]{1,0:T(4,128)}, f32[4,1152]{1,0:T(4,128)}) custom-call(f32[4]{0:T(128)} %get-tuple-element.6.a_in, f32[4,1152]{1,0:T(4,128)S(1)} %get-tuple-element.7.b_in, f32[4,1152]{1,0:T(4,128)S(1)} %get-tuple-element.8.c_in), custom_call_target="tpu_custom_call" | custom-call | tf_op jit(solution)/shard_map/pallas_call | solution.py:757

commit v5 on v4

--- a/solution.py
+++ b/solution.py
@@ -341,44 +341,42 @@
             rank = rank + same.astype(jnp.int32)
         return jnp.minimum(rank, 1)
 
-    m2_copies = []
-    for k in range(NP):
-        row = []
-        for e in (2, 1, 3, 0):
-            for half in range(2):
-                j = tile_at(e, 0) if half == 0 else tile_at(0, e)
-                owner = req_smem[j, 0, 4 * k]
-                rank = rank_of(j, k)
-                if half == 0:
-                    o = (z - (owner & 3)) & 3
-                else:
-                    o = (x - (owner >> 2)) & 3
+    m2_copies = [[] for _ in range(NP)]
+    order = [(k, e) for k in range(NP) for e in (2, 1, 3)] + [(k, 0) for k in range(NP)]
+    for k, e in order:
+        for half in range(2):
+            j = tile_at(e, 0) if half == 0 else tile_at(0, e)
+            owner = req_smem[j, 0, 4 * k]
+            rank = rank_of(j, k)
+            if half == 0:
+                o = (z - (owner & 3)) & 3
+            else:
+                o = (x - (owner >> 2)) & 3
+            if e:
+                dst = m2_send.at[half * 4 + e, k]
+            else:
+                dst = m2_recv[k].at[half, 0]
+            dst[0:8] = m1_recv[half, o, pl.ds((2 * e + rank) * 8, 8)]
+            if half == 0:
+                tile = m1_recv[0, o, 64].astype(F32)
                 if e:
-                    dst = m2_send.at[half * 4 + e, k]
-                else:
-                    dst = m2_recv[k].at[half, 0]
-                dst[0:8] = m1_recv[half, o, pl.ds((2 * e + rank) * 8, 8)]
-                if half == 0:
-                    tile = m1_recv[0, o, 64].astype(F32)
-                    if e:
-                        tile = pltpu.roll(tile, C - 2 * e * SIDE, axis=1)
-                    second = jnp.full(tile.shape, rank, jnp.int32) != 0
-                    tile = jnp.where(second, pltpu.roll(tile, C - SIDE, axis=1), tile)
-                    dst[8] = tile.astype(BF16)
-                if e:
-                    units = 9 - half
-                    n = half * 16 + e * 4 + k
-                    copy = remote(
-                        m2_send.at[half * 4 + e, k, pl.ds(0, units)],
-                        m2_recv[k].at[half, e, pl.ds(0, units)],
-                        m2_ssem.at[n],
-                        m2_rsem.at[n],
-                        j,
-                        me_d,
-                    )
-                    copy.start()
-                    row.append(copy)
-        m2_copies.append(row)
+                    tile = pltpu.roll(tile, C - 2 * e * SIDE, axis=1)
+                second = jnp.full(tile.shape, rank, jnp.int32) != 0
+                tile = jnp.where(second, pltpu.roll(tile, C - SIDE, axis=1), tile)
+                dst[8] = tile.astype(BF16)
+            if e:
+                units = 9 - half
+                n = half * 16 + e * 4 + k
+                copy = remote(
+                    m2_send.at[half * 4 + e, k, pl.ds(0, units)],
+                    m2_recv[k].at[half, e, pl.ds(0, units)],
+                    m2_ssem.at[n],
+                    m2_rsem.at[n],
+                    j,
+                    me_d,
+                )
+                copy.start()
+                m2_copies[k].append(copy)
 
     sib = me_d ^ 1
     pair_copies = []
@@ -542,14 +540,13 @@
 
     s1_copies = [[], [], []]
 
+    def put(chunk, total):
+        mine[chunk] = total.reshape(AX, AX, AX, 8, PART)
+
+    def add(chunk, total):
+        mine[chunk] = mine[chunk] + total.reshape(AX, AX, AX, 8, PART)
+
     def step1(chunk):
-        if chunk == 0:
-            total = gradient(chunk, 0, 2 * NP - 1)
-            sibling_columns(NP - 1)
-            total = total + gradient(chunk, 2 * NP - 1, 1)
-        else:
-            total = gradient(chunk, 0, 2 * NP)
-        mine[chunk] = total.reshape(AX, AX, AX, 8, PART)
         for o in (2, 1, 3):
             for part in range(3):
                 tile, dp, at = along(orders[part][0], o)
@@ -561,8 +558,14 @@
                 copy.start()
                 s1_copies[part].append(copy)
 
-    for chunk in range(3):
+    for chunk in range(2):
+        put(chunk, gradient(chunk, 0, 2 * NP - 1))
+    sibling_columns(NP - 1)
+    for chunk in range(2):
+        add(chunk, gradient(chunk, 2 * NP - 1, 1))
         step1(chunk)
+    put(2, gradient(2, 0, 2 * NP))
+    step1(2)
 
     def piece2(part, at):
         return tot2[part, :, at] if part == 1 else tot2[part, at]

time: 70.3 us -> 69.6 us (0.990)
  no operation moved by 1% of the time
where the time goes in v5:
time: 69.6 us; the launch traced here: 69.5 us
  Pallas kernels  68.8 us (99%)
    pallas_call x1, Pallas kernels, local(): pl.pallas_call(kernel, out_shape=(outs[0], pltpu.VMEM((4, WIDE), F32), pl...  67.7 us

profile of v5, /device:TPU:1, one launch (start us, length us, event | category | flops | bytes accessed | tf_op | source)
XLA Modules:
  0.0 69.5 jit_solution(11049030537683955583)
XLA Ops:
  0.6 67.7 %shard_map.166 = (f32[4]{0:T(128)}, f32[4,1152]{1,0:T(4,128)S(1)}, f32[4,1152]{1,0:T(4,128)S(1)}) custom-call(bf16[64,256,128]{2,1,0:T(8,128)(2,1)} %feat_hbm.1, bf16[64,256]{1,0:T(8,128)(2,1)} %tgt_hbm.1, s32[4]{0:T(128)} %bitcast.1, s32[4]{0:T(128)} %row_hbm.1, s32[4]{0:T(128)} %col_hbm.1, s32[4]{0:T(128)} %level_hbm.1, s32[4]{0:T(128)} %count_hbm.1, ...), custom_call_target="tpu_custom_call" | custom-call | tf_op jit(solution)/shard_map/pallas_call | solution.py:750
  68.3 1.1 %shard_map.167 = (f32[4]{0:T(128)}, f32[4,1152]{1,0:T(4,128)}, f32[4,1152]{1,0:T(4,128)}) custom-call(f32[4]{0:T(128)} %get-tuple-element.6.a_in, f32[4,1152]{1,0:T(4,128)S(1)} %get-tuple-element.7.b_in, f32[4,1152]{1,0:T(4,128)S(1)} %get-tuple-element.8.c_in), custom_call_target="tpu_custom_call" | custom-call | tf_op jit(solution)/shard_map/pallas_call | solution.py:760

commit v6 on v5

--- a/solution.py
+++ b/solution.py
@@ -172,6 +172,18 @@
 
     m2_recv = (m2_recv0, m2_recv1, m2_recv2, m2_recv3)
 
+    leaving = []
+
+    def arrive(copies):
+        for copy in copies:
+            copy.wait_recv()
+        leaving.extend(copies)
+
+    def settle():
+        for copy in leaving:
+            copy.wait_send()
+        leaving.clear()
+
     barrier = pltpu.get_barrier_semaphore()
     staged = []
 
@@ -243,8 +255,7 @@
         feat_f[2 * i] = feat_v[2 * i].astype(F32)
         feat_f[2 * i + 1] = feat_v[2 * i + 1].astype(F32)
 
-    for copy in copies:
-        copy.wait()
+    arrive(copies)
     to_smem = pltpu.make_async_copy(req_recv, req_smem, local_sem.at[len(staged)])
     to_smem.start()
     to_smem.wait()
@@ -308,6 +319,7 @@
             m1_copies[half].append(copy)
     for half in range(2):
         fill(half, 0, m1_recv.at[half, 0])
+    settle()
 
     for copy in small:
         copy.wait()
@@ -331,8 +343,7 @@
     noise_v[:, :, 0:SIDE] = noise_b[...]
 
     for half in range(2):
-        for copy in m1_copies[half]:
-            copy.wait()
+        arrive(m1_copies[half])
 
     def rank_of(j, k):
         rank = jnp.int32(0)
@@ -378,6 +389,8 @@
                 copy.start()
                 m2_copies[k].append(copy)
 
+    settle()
+
     sib = me_d ^ 1
     pair_copies = []
     wo = wo_ref[...].reshape(1, 1, C)
@@ -386,8 +399,7 @@
     col3, lane3 = iota(shape3, 1), iota(shape3, 2)
     none = jnp.zeros((1, SIDE, C), F32)
     for p in range(NP):
-        for copy in m2_copies[p]:
-            copy.wait()
+        arrive(m2_copies[p])
         owner = owner_ref[p]
         from_x, from_z = (x - (owner >> 2)) & 3, (z - (owner & 3)) & 3
         blk[0:8] = m2_recv[p][0, from_x, 0:8]
@@ -491,8 +503,7 @@
         pair_copies.append(row)
 
     def sibling_columns(p):
-        for copy in pair_copies[p]:
-            copy.wait()
+        arrive(pair_copies[p])
         dst = right.at[core]
         for s, moved in enumerate(column_shifts(raw_recv[p].astype(F32))):
             rows = moved.astype(BF16)
@@ -504,15 +515,12 @@
     for p in range(NP - 1):
         sibling_columns(p)
 
-    def gradient(chunk, first, count):
+    def gradient(tile, tiles, first, count):
         return lax.dot_general(
             left[core, first * CELLS : (first + count) * CELLS],
             right[
-                core,
-                first * SIDE : (first + count) * SIDE,
-                :,
-                chunk * PART : (chunk + 1) * PART,
-            ].reshape(count * CELLS, PART),
+                core, first * SIDE : (first + count) * SIDE, :, tile * C : (tile + tiles) * C
+            ].reshape(count * CELLS, tiles * C),
             (((0,), (0,)), ((), ())),
             preferred_element_type=F32,
         )
@@ -540,11 +548,14 @@
 
     s1_copies = [[], [], []]
 
-    def put(chunk, total):
-        mine[chunk] = total.reshape(AX, AX, AX, 8, PART)
-
-    def add(chunk, total):
-        mine[chunk] = mine[chunk] + total.reshape(AX, AX, AX, 8, PART)
+    def put(tile, tiles, total, more):
+        total = total.reshape(AX, AX, AX, 8, tiles * C)
+        for i in range(tiles):
+            chunk, part = (tile + i) // 3, (tile + i) % 3
+            at = (chunk, slice(None), slice(None), slice(None), slice(None))
+            at = at + (slice(part * C, (part + 1) * C),)
+            piece = total[..., i * C : (i + 1) * C]
+            mine[at] = mine[at] + piece if more else piece
 
     def step1(chunk):
         for o in (2, 1, 3):
@@ -558,13 +569,15 @@
                 copy.start()
                 s1_copies[part].append(copy)
 
-    for chunk in range(2):
-        put(chunk, gradient(chunk, 0, 2 * NP - 1))
+    last = 2 * NP - 1
+    put(0, 4, gradient(0, 4, 0, last), False)
+    put(4, 2, gradient(4, 2, 0, last), False)
     sibling_columns(NP - 1)
-    for chunk in range(2):
-        add(chunk, gradient(chunk, 2 * NP - 1, 1))
-        step1(chunk)
-    put(2, gradient(2, 0, 2 * NP))
+    put(0, 4, gradient(0, 4, last, 1), True)
+    step1(0)
+    put(4, 2, gradient(4, 2, last, 1), True)
+    step1(1)
+    put(6, 3, gradient(6, 3, 0, last + 1), False)
     step1(2)
 
     def piece2(part, at):
@@ -572,8 +585,7 @@
 
     s2_copies = []
     for part in range(3):
-        for copy in s1_copies[part]:
-            copy.wait()
+        arrive(s1_copies[part])
         for chunk in range(3):
             total = piece1(chunk, part, here[orders[part][0]])
             for o in range(3):
@@ -590,10 +602,11 @@
             row.append(copy)
         s2_copies.append(row)
 
+    settle()
+
     s3_copies = []
     for part in range(3):
-        for copy in s2_copies[part]:
-            copy.wait()
+        arrive(s2_copies[part])
         total = piece2(part, here[orders[part][1]])
         for o in range(3):
             total = total + s2_recv[part * 3 + o].astype(F32).reshape(AX, 8, PART)
@@ -609,10 +622,10 @@
             row.append(copy)
         s3_copies.append(row)
 
+    settle()
     squares = jnp.zeros((8, C), F32)
     for part in range(3):
-        for copy in s3_copies[part]:
-            copy.wait()
+        arrive(s3_copies[part])
         total = tot3[part, here[orders[part][2]]]
         for o in range(3):
             total = total + s3_recv[part * 3 + o]
@@ -630,8 +643,8 @@
         copies.append(copy)
     fin_copy = remote(fin.at[0], fin.at[1], fin_sem.at[0], fin_sem.at[1], me_t, sib)
     fin_copy.start()
-    for copy in copies:
-        copy.wait()
+    settle()
+    arrive(copies)
     plane = jnp.sum(nrm_recv[...], axis=0)
     nrm2_send[...] = plane
     nrm2_recv[me_d] = plane
@@ -642,9 +655,9 @@
         )
         copy.start()
         copies.append(copy)
-    fin_copy.wait()
-    for copy in copies:
-        copy.wait()
+    settle()
+    arrive([fin_copy, *copies])
+    settle()
 
     total_a = jnp.sum(nrm2_recv[0] + nrm2_recv[2] + nrm2_recv[4] + nrm2_recv[6], keepdims=True)
     total_b = jnp.sum(nrm2_recv[1] + nrm2_recv[3] + nrm2_recv[5] + nrm2_recv[7], keepdims=True)

time: 69.6 us -> 69.3 us (level)
  no operation moved by 1% of the time
where the time goes in v6:
time: 69.3 us; the launch traced here: 69.2 us
  Pallas kernels  68.5 us (99%)
    pallas_call x1, Pallas kernels, local(): pl.pallas_call(kernel, out_shape=(outs[0], pltpu.VMEM((4, WIDE), F32), pl...  67.4 us

profile of v6, /device:TPU:1, one launch (start us, length us, event | category | flops | bytes accessed | tf_op | source)
XLA Modules:
  0.0 69.2 jit_solution(10094822752976530604)
XLA Ops:
  0.6 67.4 %shard_map.166 = (f32[4]{0:T(128)}, f32[4,1152]{1,0:T(4,128)S(1)}, f32[4,1152]{1,0:T(4,128)S(1)}) custom-call(bf16[64,256,128]{2,1,0:T(8,128)(2,1)} %feat_hbm.1, bf16[64,256]{1,0:T(8,128)(2,1)} %tgt_hbm.1, s32[4]{0:T(128)} %bitcast.1, s32[4]{0:T(128)} %row_hbm.1, s32[4]{0:T(128)} %col_hbm.1, s32[4]{0:T(128)} %level_hbm.1, s32[4]{0:T(128)} %count_hbm.1, ...), custom_call_target="tpu_custom_call" | custom-call | tf_op jit(solution)/shard_map/pallas_call | solution.py:763
  68.0 1.1 %shard_map.167 = (f32[4]{0:T(128)}, f32[4,1152]{1,0:T(4,128)}, f32[4,1152]{1,0:T(4,128)}) custom-call(f32[4]{0:T(128)} %get-tuple-element.6.a_in, f32[4,1152]{1,0:T(4,128)S(1)} %get-tuple-element.7.b_in, f32[4,1152]{1,0:T(4,128)S(1)} %get-tuple-element.8.c_in), custom_call_target="tpu_custom_call" | custom-call | tf_op jit(solution)/shard_map/pallas_call | solution.py:773
